TPU v7x, 256 devices: a whole 4x4x8 slice. The times are simulated.
256 devices in a mesh: ctx: 32 (over y, z), tp: 8 (over x, core).
Axes of the slice: x: 4, y: 4, z: 8, core: 2. Of those that a mesh axis runs over, the one named last changes fastest.
Arguments:
- streams: bfloat16 [3, 4096, 8192], P(None, 'ctx', 'tp'), may hold values from -6 to 6
- short_filter: float32 [3, 7, 512], P(None, None, 'tp'), may hold values from -2.5 to 2.5
- residues: float32 [16, 512], P(None, 'tp'), may hold values from -0.125 to 0.125
- rates: float32 [16, 512], P(None, 'tp'), may hold values from 2.4414062e-06 to 0.04
- skip: float32 [8192], P('tp'), may hold values from 0.5 to 1.5
- out_weight: bfloat16 [4096, 8192], P('ctx', 'tp'), may hold values from -0.0625 to 0.0625
- out_cotangent: bfloat16 [4096, 4096], P('ctx', 'tp'), may hold values from -12 to 12
Outputs:
- output: bfloat16 [4096, 4096], P('ctx', 'tp')
- grad_streams: bfloat16 [3, 4096, 8192], P(None, 'ctx', 'tp')
- grad_short: float32 [3, 7, 512], P(None, None, 'tp')
- grad_skip: float32 [8192], P('tp')
- grad_weight: float32 [4096, 8192], P('ctx', 'tp')
All inputs are finite; a program needn't handle non-finite values.
Results may differ from a plain program's by a relative error of at most 0.034.
Values may be sent and summed in bfloat16 or wider, within the bound.
A program may use at most 128 MiB of HBM per device.

v0:
```python
import jax
import jax.numpy as jnp
from jax import lax
from jax.sharding import PartitionSpec as P

BLOCK = 256


highest = lax.Precision.HIGHEST


def entering_2(part, axis, combine, identity, reverse):
    count = lax.axis_size(axis)
    place = lax.axis_index(axis)
    ahead = count - 1 - place if reverse else place
    gathered = jax.tree.map(lambda a: lax.all_gather(a, axis), part)
    state = jax.tree.map(lambda a, e: jnp.zeros_like(a) + jnp.asarray(e, a.dtype), part, identity)

    def one(hop, state):
        source = count - 1 - hop if reverse else hop
        return combine(
            state, jax.tree.map(lambda a: lax.dynamic_index_in_dim(a, source, 0, False), gathered)
        )

    return lax.fori_loop(0, ahead, one, state)


def passed_along(block, axis, distance):
    devices = range(lax.axis_size(axis))
    route = [(i - distance, i) for i in devices if i - distance in devices]
    return lax.ppermute(block, axis, route)


def modal_tables(residues, rates, length, row_count):
    positions = jnp.arange(length, dtype=jnp.float32)
    profile = jnp.sum(
        residues[:, None, :] * jnp.exp(-rates[:, None, :] * positions[None, :, None]), axis=0
    )
    counter = jnp.arange(length, dtype=jnp.int32)
    offset = counter[:, None] - counter[None, :]
    toeplitz = jnp.where(
        (offset >= 0)[:, :, None], jnp.take(profile, jnp.maximum(offset, 0), axis=0), 0.0
    )
    inflow = jnp.exp(-rates[None] * (length - 1.0 - positions)[:, None, None])
    carried = residues[None] * jnp.exp(-rates[None] * (positions + 1.0)[:, None, None])
    block_decay = jnp.exp(-rates * length)
    places = jnp.arange(row_count, dtype=jnp.float32)
    entering = residues[None] * jnp.exp(-rates[None] * (places + 1.0)[:, None, None])
    device_decay = jnp.exp(-rates * row_count)
    return (toeplitz, inflow, carried, block_decay, entering, device_decay)


def local_pass(source, toeplitz, inflow, carried, block_decay):
    state = jnp.zeros((inflow.shape[1],) + source.shape[1:], jnp.float32)
    local = jnp.einsum("tsg,sgc->tgc", toeplitz, source, precision=highest)
    local = local + jnp.einsum("tmg,mgc->tgc", carried, state, precision=highest)
    state = block_decay[:, :, None] * state + jnp.einsum(
        "smg,sgc->mgc", inflow, source, precision=highest
    )
    return (local, state)


def combine(earlier, later):
    return (earlier[0] * later[0], later[0][:, :, None] * earlier[1] + later[1])


def states_before(ending, device_decay):
    neutral = (jnp.ones_like(device_decay), jnp.zeros_like(ending))
    result = entering_2((device_decay, ending), "ctx", combine, neutral, False)[1]
    return result


def states_after(ending, device_decay):
    neutral = (jnp.ones_like(device_decay), jnp.zeros_like(ending))
    result = entering_2((device_decay, ending), "ctx", combine, neutral, True)[1]
    return result


def shards(streams, short_filter, residues, rates, skip, out_weight, out_cotangent):
    row_count = streams.shape[1]
    channels = streams.shape[2]
    groups = residues.shape[1]
    members = channels // groups
    reach = short_filter.shape[1] - 1
    length = min(BLOCK, row_count)
    taps = jnp.repeat(short_filter, members, axis=2)
    rim = passed_along(streams[:, row_count - reach :, :], "ctx", 1)
    padded = jnp.concatenate([rim, streams], axis=1)
    smoothed = jnp.zeros(streams.shape, jnp.float32)
    for lag in range(reach + 1):
        smoothed = smoothed + taps[:, lag, None, :] * padded[
            :, reach - lag : reach - lag + row_count, :
        ].astype(jnp.float32)
    mixed = lax.optimization_barrier((smoothed[1] * smoothed[2]).astype(jnp.bfloat16)).astype(
        jnp.float32
    )
    toeplitz, inflow, carried, block_decay, entering, device_decay = modal_tables(
        residues, rates, length, row_count
    )
    local, ending = local_pass(
        mixed.reshape(row_count, groups, members), toeplitz, inflow, carried, block_decay
    )
    before = states_before(ending, device_decay)
    long_part = local + jnp.einsum("tmg,mgc->tgc", entering, before, precision=highest)
    field = long_part.reshape(row_count, channels) + skip * mixed
    gated = (smoothed[0] * field).astype(jnp.bfloat16)
    weights = lax.all_gather(out_weight, "ctx", axis=0, tiled=True)
    partial_value = lax.dot_general(
        gated, weights, (((1,), (1,)), ((), ())), preferred_element_type=jnp.float32
    )
    output = lax.psum_scatter(
        partial_value.astype(jnp.bfloat16), "tp", scatter_dimension=1, tiled=True
    )
    cotangent = lax.all_gather(out_cotangent, "tp", axis=1, tiled=True)
    upstream = jnp.dot(cotangent, weights, preferred_element_type=jnp.float32)
    grad_weight = lax.psum_scatter(
        lax.dot_general(
            cotangent, gated, (((0,), (0,)), ((), ())), preferred_element_type=jnp.float32
        ).astype(jnp.bfloat16),
        "ctx",
        scatter_dimension=0,
        tiled=True,
    ).astype(jnp.float32)
    grad_field = upstream * smoothed[0]
    skip_part = jnp.sum(grad_field * mixed, axis=0)
    flipped = grad_field[::-1].reshape(row_count, groups, members)
    back_local, back_end = local_pass(flipped, toeplitz, inflow, carried, block_decay)
    after = states_after(back_end, device_decay)
    back_part = back_local + jnp.einsum("tmg,mgc->tgc", entering, after, precision=highest)
    grad_mixed = back_part.reshape(row_count, channels)[::-1] + skip * grad_field
    grad_smoothed = jnp.stack(
        [upstream * field, grad_mixed * smoothed[2], grad_mixed * smoothed[1]]
    )
    tap_rows = []
    for lag in range(reach + 1):
        product = grad_smoothed * padded[:, reach - lag : reach - lag + row_count, :].astype(
            jnp.float32
        )
        tap_rows.append(jnp.sum(product.reshape(3, row_count, groups, members), axis=(1, 3)))
    tap_part = jnp.stack(tap_rows, axis=1)
    grad_skip, grad_short = lax.psum((skip_part, tap_part), "ctx")
    rim_next = passed_along(grad_smoothed[:, :reach, :], "ctx", -1)
    padded_back = jnp.concatenate([grad_smoothed, rim_next], axis=1)
    grad_streams = jnp.zeros(streams.shape, jnp.float32)
    for lag in range(reach + 1):
        grad_streams = (
            grad_streams + taps[:, lag, None, :] * padded_back[:, lag : lag + row_count, :]
        )
    return (output, grad_streams.astype(jnp.bfloat16), grad_short, grad_skip, grad_weight)


def solution(mesh):
    return jax.shard_map(
        shards,
        mesh=mesh,
        in_specs=(
            P(None, "ctx", "tp"),
            P(None, None, "tp"),
            P(None, "tp"),
            P(None, "tp"),
            P("tp"),
            P("ctx", "tp"),
            P("ctx", "tp"),
        ),
        out_specs=(
            P("ctx", "tp"),
            P(None, "ctx", "tp"),
            P(None, None, "tp"),
            P("tp"),
            P("ctx", "tp"),
        ),
        check_vma=False,
    )
```

profile of v0, /device:TPU:4, one launch (start us, length us, event | category | flops | bytes accessed | tf_op | source)
XLA Modules:
  0.0 592.7 jit_solution(405877520974136037)
XLA Ops:
  8.1 3.8 collective-permute-start
  13.7 1.5 fusion.15
  19.2 54.5 %gather_fusion = f32[16384,64]{1,0:T(8,128)} fusion(f32[128,64]{1,0:T(8,128)S(1)} %copy.60, s32[16384]{0:T(1024)S(1)} %bitcast_clamp_fusion), kind=kCustom, calls=%fused_computation | custom fusion | bytes 8454144 | tf_op jit(solution)/shard_map/jit(_take)/gather | solution.py:42
  73.7 7.4 %copy.61 = f32[128,128,64]{1,0,2:T(8,128)} copy(f32[128,128,64]{2,1,0:T(8,128)} %bitcast.109) | data formatting | bytes 8388608 | tf_op jit(solution)/shard_map/jit(_take)/gather | solution.py:42
  81.1 53.3 %all-gather = f32[512,64]{1,0:T(8,128)S(1)} all-gather(f32[16,64]{1,0:T(8,128)S(1)} %get-tuple-element.212), channel_id=2, replica_groups=mesh['ctx'=32,'tp'=8] {'ctx'}, dimensions={0}, use_global_device_ids=true | all-gather | bytes 135168 | tf_op jit(solution)/shard_map/all_gather | solution.py:16
  136.1 6.4 %fusion.31 = f32[64,16,128]{2,1,0:T(8,128)} fusion(f32[64,16,128]{2,1,0:T(8,128)S(1)} %fusion.41, bf16[128,64,16]{0,2,1:T(8,128)(2,1)S(1)} %bitcast.113, f32[128,128,64]{1,0,2:T(8,128)} %copy.61, pred[128,128]{1,0:T(8,128)(4,1)S(1)} %get-tuple-element.220, pred[128,128]{1,0:T(8,128)(4,1)S(1)} %get-tuple-element.221), kind=kOutput, calls=%fused_computation.69 | convolution fusion | flops 203554816 | bytes 5537792 | tf_op jit(solution)/shard_map/tsg,sgc->tgc/dot_general | solution.py:55
  143.1 2.7 convolution_add_fusion.1
  145.7 2.0 copy.68
  147.8 81.9 %all-gather.8.cloned.1.call-done = bf16[4096,1024]{1,0:T(8,128)(2,1)} async-done(((bf16[128,1024]{1,0:T(8,128)(2,1)}), bf16[4096,1024]{1,0:T(8,128)(2,1)}) %all-gather.8.cloned.1.call-update) | async-done | bytes 8388624 | tf_op jit(solution)/shard_map/all_gather | solution.py:107
  229.7 5.7 fusion.40
  236.2 2.6 rev.6
  238.8 2.1 copy.69
  240.9 2.9 fusion.32
  243.8 1.9 copy.70
  245.8 5.6 convert_bitcast_fusion
  251.4 12.0 %copy.75 = bf16[4096,1024]{1,0:T(8,128)(2,1)} copy(bf16[4096,1024]{0,1:T(8,128)(2,1)} %convert_bitcast_fusion) | data formatting | bytes 16777216
  264.6 9.0 %fusion.30 = f32[64,16,128]{2,1,0:T(8,128)} fusion(f32[64,16,128]{2,1,0:T(8,128)S(1)} %copy-done.6, f32[128,64,16]{0,2,1:T(8,128)S(1)} %bitcast.111, f32[128,128,64]{1,0,2:T(8,128)} %copy.61, pred[128,128]{1,0:T(8,128)(4,1)S(1)} %copy-done.23, pred[128,128]{1,0:T(8,128)(4,1)S(1)} %copy-done.25), kind=kOutput, calls=%fused_computation.65 | convolution fusion | flops 203554816 | bytes 5799936 | tf_op jit(solution)/shard_map/tsg,sgc->tgc/dot_general | solution.py:55
  273.6 7.3 %convolution_convert_fusion = bf16[128,4096]{1,0:T(8,128)(2,1)} fusion(bf16[128,1024]{1,0:T(8,128)(2,1)S(1)} %get-tuple-element.202, bf16[4096,1024]{1,0:T(8,128)(2,1)} %all-gather.8.cloned.1.call-done), kind=kOutput, calls=%fused_computation.6 | convolution fusion | flops 1074266112 | bytes 9699328 | tf_op jit(solution)/shard_map/dot_general | solution.py:108
  280.9 43.8 %all-gather.14.cloned.1.call-done = f32[512,64,16]{1,2,0:T(8,128)} async-done(((f32[16,64,16]{1,2,0:T(8,128)}), f32[512,64,16]{1,2,0:T(8,128)}) %all-gather.14.cloned.1.call-update) | async-done | bytes 2097168 | tf_op jit(solution)/shard_map/all_gather | solution.py:16
  324.7 52.4 %while.27 = (s32[]{:T(128)}, f32[16,64,16]{1,2,0:T(8,128)S(1)}, s32[]{:T(128)}, f32[32,16,64]{2,1,0:T(8,128)}, f32[32,16,64,16]{2,3,1,0:T(8,128)}, /*index=5*/s32[]{:T(128)}, s32[]{:T(128)}, s32[]{:T(128)}, s32[]{:T(128)}) while((s32[]{:T(128)}, f32[16,64,16]{1,2,0:T(8,128)S(1)}, s32[]{:T(128)}, f32[32,16,64]{2,1,0:T(8,128)}, ...), condition=%wide.region_5.6_spmd, body=%wide.region_4.5_spmd.sunk | while | flops 32774 | bytes 209051 | solution.py:25
  337.2 1.0 bitcast_add_fusion.5
  377.5 2.6 convolution_add_fusion
  380.1 1.2 copy.72
  381.4 2.6 rev.7
  384.0 1.4 multiply_bitcast_fusion.1
  385.6 1.4 collective-permute-start.1
  387.0 1.7 fusion.21
  390.3 140.8 %all-reduce = (f32[3,7,64]{2,0,1:T(4,128)S(1)}, f32[1024]{0:T(1024)}) all-reduce(f32[3,7,64]{2,0,1:T(4,128)S(1)} %constant_dynamic-update-slice_fusion, f32[1024]{0:T(1024)S(1)} %copy-done.28), channel_id=1, replica_groups=mesh['ctx'=32,'tp'=8] {'ctx'}, use_global_device_ids=true, to_apply=%region_20.21 | all-reduce | flops 2368 | bytes 18944 | tf_op jit(solution)/shard_map/psum | solution.py:141
  532.5 2.2 fusion.24
  534.7 20.1 %reduce-scatter.7.cloned.1.call-done = bf16[128,1024]{1,0:T(8,128)(2,1)} async-done(((bf16[4096,1024]{1,0:T(8,128)(2,1)}), bf16[128,1024]{1,0:T(8,128)(2,1)}) %reduce-scatter.7.cloned.1.call-update) | async-done | bytes 262160
  554.8 1.1 copy.76
  556.8 29.0 %reduce-scatter.5.cloned.1.call-done = bf16[128,512]{1,0:T(8,128)(2,1)} async-done(((bf16[128,4096]{1,0:T(8,128)(2,1)}), bf16[128,512]{1,0:T(8,128)(2,1)}) %reduce-scatter.5.cloned.1.call-update) | async-done | bytes 131088 | tf_op jit(solution)/shard_map/reduce_scatter | solution.py:111
  (199 shorter events, 65.4 us)
Async XLA Ops:
  7.2 6.5 %copy-start.3 = (bf16[3,128,1024]{2,1,0:T(8,128)(2,1)S(1)}, bf16[3,128,1024]{2,1,0:T(8,128)(2,1)}, u32[]{:S(2)}) copy-start(bf16[3,128,1024]{2,1,0:T(8,128)(2,1)} %param.11) | copy-start | bytes 2359300
  7.2 6.2 %copy-start.30 = (f32[16,64]{1,0:T(8,128)S(1)}, f32[16,64]{1,0:T(8,128)}, u32[]{:S(2)}) copy-start(f32[16,64]{1,0:T(8,128)} %param.14) | copy-start | bytes 12292
  7.2 135.3 %all-gather.12.cloned.1.call-start = ((), (), s32[]{:S(2)}) async-start(), calls=%async_computation.5 | async-start | bytes 4325376 | tf_op jit(solution)/shard_map/all_gather | solution.py:16
  8.1 5.6 collective-permute-start
  13.4 1.9 copy-start.8
  13.4 1.9 copy-start.10
  13.4 1.9 copy-start.12
  13.4 1.9 copy-start.14
  13.4 1.8 copy-start.16
  13.5 1.8 copy-start.18
  13.5 2.0 copy-start.33
  13.5 1.8 copy-start.20
  15.3 3.3 copy-start.29
  17.1 130.7 %all-gather.10.cloned.1.call-start = ((), (), s32[]{:S(2)}) async-start(), calls=%async_computation.4 | async-start | bytes 1179648 | tf_op jit(solution)/shard_map/all_gather | solution.py:114
  17.9 211.8 %all-gather.8.cloned.1.call-start = ((), (), s32[]{:S(2)}) async-start(), calls=%async_computation.2 | async-start | bytes 8650752 | tf_op jit(solution)/shard_map/all_gather | solution.py:107
  18.6 306.1 %all-gather.14.cloned.1.call-start = ((), (), s32[]{:S(2)}) async-start(), calls=%async_computation.6 | async-start | bytes 4325376 | tf_op jit(solution)/shard_map/all_gather | solution.py:16
  134.4 8.6 %copy-start.31 = (f32[128]{0:T(128)}, f32[128]{0:T(128)S(1)}, u32[]{:S(2)}) copy-start(f32[128]{0:T(128)S(1)} %iota_add_fusion) | copy-start | bytes 1540
  134.5 0.8 copy-start.22
  142.7 5.0 copy-start.7
  142.7 86.9 %copy-start.26 = (f32[1024]{0:T(1024)S(1)}, f32[1024]{0:T(1024)}, u32[]{:S(2)}) copy-start(f32[1024]{0:T(1024)} %param.15) | copy-start | bytes 12292
  238.8 7.0 %copy-start = (bf16[128,4096]{1,0:T(8,128)(2,1)S(1)}, bf16[128,4096]{1,0:T(8,128)(2,1)}, u32[]{:S(2)}) copy-start(bf16[128,4096]{1,0:T(8,128)(2,1)} %all-gather.10.cloned.1.call-done) | copy-start | bytes 3145732
  245.7 309.1 %reduce-scatter.7.cloned.1.call-start = ((), (), s32[]{:S(2)}) async-start(), calls=%async_computation.7 | async-start | bytes 8650752
  263.4 1.0 copy-start.2
  263.4 1.2 copy-start.6
  263.4 1.2 copy-start.23
  263.4 1.2 copy-start.25
  263.5 322.4 %reduce-scatter.5.cloned.1.call-start = ((), (), s32[]{:S(2)}) async-start(), calls=%async_computation.3 | async-start | bytes 1179648 | tf_op jit(solution)/shard_map/reduce_scatter | solution.py:111
  280.9 96.5 %copy-start.32 = (f32[128]{0:T(128)S(1)}, f32[128]{0:T(128)}, u32[]{:S(2)}) copy-start(f32[128]{0:T(128)} %copy-done.31) | copy-start | bytes 1540
  377.5 6.5 %copy-start.27 = (f32[1024]{0:T(1024)S(1)}, f32[1024]{0:T(1024)}, u32[]{:S(2)}) copy-start(f32[1024]{0:T(1024)} %param.15) | copy-start | bytes 12292
  385.4 1.6 copy-start.4
  385.6 4.7 copy-start.28
  385.6 146.1 %collective-permute-start.1 = (f32[3,6,1024]{2,1,0:T(8,128)S(1)}, f32[3,6,1024]{2,1,0:T(8,128)S(1)}, u32[]{:S(2)}, u32[]{:S(2)}) collective-permute-start(f32[3,6,1024]{2,1,0:T(8,128)S(1)} %slice.134), channel_id=1, source_target_pairs={{8,0},{16,8},{24,16},{32,24},{40,32},{48,40},{56,48},{64,56},{72,6... | collective-permute-start | bytes 221192 | tf_op jit(solution)/shard_map/ppermute | solution.py:31
  (10 other events, 7.8 us)
Sparse Core Ops, SparseCore 0:
  17.2 86.3 all-gather.11
  105.4 21.7 all-gather.9
  129.8 99.7 all-gather.7
  245.8 78.8 all-gather.13
  328.6 226.1 reduce-scatter.6
  557.9 27.8 reduce-scatter.4
where the time goes:
time: 600 us; the launch traced here: 593 us
  blocking collectives  194 us (32%)
  waiting for transfers between devices  176 us (29%)
  local copies, waits for them, and re-layouts  119 us (20%)
  matrix products  43.5 us (7%)
  other arithmetic  38 us (6%)
  between operations  14.8 us (2%)
    psum x1, blocking collectives, shards(): grad_skip, grad_short = lax.psum((skip_part, tap_part), 'ctx')  141 us
    all_gather x1, waiting for transfers between devices, shards(): weights = lax.all_gather(out_weight, 'ctx', axis=0, tiled=True)  81.9 us
    gather x2, local copies, waits for them, and re-layouts, modal_tables(): jnp.take(profile, jnp.maximum(offset, 0), axis=0)  61.9 us
    all_gather x1, blocking collectives, entering_2(): gathered = jax.tree.map(lambda a: lax.all_gather(a, axis), part)  53.3 us
    all_gather x2, waiting for transfers between devices, entering_2(): gathered = jax.tree.map(lambda a: lax.all_gather(a, axis), part)  43.8 us
    add x31, other arithmetic, combine(): return (earlier[0] * later[0], later[0][:, :, None] * earlier[1] + later[1])  29.7 us
    reduce_scatter x1, waiting for transfers between devices, shards(): lax.psum_scatter(partial_value.astype(jnp.bfloat16), 'tp', scatter_dimens...  29 us
    mul x31, local copies, waits for them, and re-layouts, combine(): return (earlier[0] * later[0], later[0][:, :, None] * earlier[1] + later[1])  21.8 us
  transfers between devices with their start and end apart: 8, of which 4 were waited for; matrix products, arithmetic and copies ran while one was open for 30% of the time, Pallas kernels for 0%

commit v1 on v0

v1 whole, which is shorter than its diff:
```python
import functools

import jax
import jax.numpy as jnp
from jax import lax
from jax.experimental import pallas as pl
from jax.experimental.pallas import tpu as pltpu
from jax.sharding import PartitionSpec as P

F32 = jnp.float32
BF16 = jnp.bfloat16
HIGHEST = lax.Precision.HIGHEST
MESH = pl.DeviceIdType.MESH
ROWS = 128
LANES = 128
MEMBERS = 16
MODES = 16
TAPS = 7
PER_TILE = LANES // MEMBERS


def iota(shape, dim):
    return lax.broadcasted_iota(jnp.int32, shape, dim)


def two_terms(value):
    high = value.astype(BF16)
    return high, (value - high.astype(F32)).astype(BF16)


def kernel(
    dims,
    s_ref,
    sf_ref,
    res_ref,
    rate_ref,
    skip_ref,
    w_ref,
    cot_ref,
    out_ref,
    gs_ref,
    gshort_ref,
    gskip_ref,
    gw_ref,
    xpad,
    rim_in,
    sm,
    mixed,
    field,
    gfb,
    gm,
    tf,
    tb,
    inf,
    inb,
    entf,
    entb,
    rate_ch,
    dec,
    vecs,
    taps,
    prof,
    st_out,
    stz,
    tot,
    ret_out,
    bef,
    wg,
    cotg,
    gg,
    upp,
    up_in,
    outp,
    out_in,
    gwp,
    gw_r,
    gw_l,
    gsp,
    tapsum,
    sml,
    smz,
    smy,
    rim_sem,
    cot_s,
    cot_r,
    wr_sem,
    wl_sem,
    stz_sem,
    tot_sem,
    bef_sem,
    g_sem,
    up_sem,
    out_s,
    out_r,
    gwr_sem,
    gwl_sem,
    grim_sem,
    smz_sem,
    smy_sem,
):
    NX, NY, NZ, NK = dims
    C = s_ref.shape[2]
    G = sf_ref.shape[2]
    OT = cot_ref.shape[1]
    OY = NZ * ROWS
    R = NZ // 2
    L = NZ - 1 - R
    c = lax.axis_index("ctx")
    p = lax.axis_index("tp")
    y, z = lax.div(c, NZ), lax.rem(c, NZ)
    x, k = lax.div(p, NK), lax.rem(p, NK)
    last = NY * NZ - 1

    def dev(yy, zz, xx=x, kk=k):
        return (yy * NZ + zz, xx * NK + kk)

    def plus(a, d, n):
        return lax.rem(a + d + n, n)

    def remote(src, dst, ssem, rsem, to):
        return pltpu.make_async_remote_copy(
            src_ref=src, dst_ref=dst, send_sem=ssem, recv_sem=rsem, device_id=to, device_id_type=MESH
        )

    def rows_of(block):
        return pl.ds(pl.multiple_of(block * ROWS, ROWS), ROWS)

    def lanes_of(tile, width=LANES):
        return pl.ds(pl.multiple_of(tile * width, width), width)

    def unless_self(pair, body):
        if pair == (0, 0):
            pl.when(x != y)(body)
        else:
            body()

    pairs = [(a, b) for a in range(NX) for b in range(NK)]

    barrier = pltpu.get_barrier_semaphore()

    def greet(to):
        pl.semaphore_signal(barrier, inc=1, device_id=to, device_id_type=MESH)

    for d in range(1, NZ):
        greet(dev(y, plus(z, d, NZ)))
    for d in range(1, NY):
        greet(dev(plus(y, d, NY), z))
    for pair in pairs:
        unless_self(pair, lambda: greet(dev(x, z, plus(x, pair[0], NX), plus(k, pair[1], NK))))
        unless_self(pair, lambda: greet(dev(plus(y, pair[0], NY), z, y, plus(k, pair[1], NK))))

    @pl.when(c > 0)
    def _():
        greet((c - 1, p))

    @pl.when(c < last)
    def _():
        greet((c + 1, p))

    peers = NZ - 1 + NY - 1 + 2 * (NX * NK - 1)
    peers = peers + jnp.where(x != y, 2, 0) + jnp.where(c > 0, 1, 0) + jnp.where(c < last, 1, 0)
    pl.semaphore_wait(barrier, peers)

    rim_copy = remote(
        s_ref.at[:, pl.ds(ROWS - 16, 16), :], rim_in, rim_sem.at[0], rim_sem.at[1], (lax.rem(c + 1, last + 1), p)
    )

    @pl.when(c < last)
    def _():
        rim_copy.start()

    right, left = dev(y, plus(z, 1, NZ)), dev(y, plus(z, -1, NZ))
    wg[rows_of(z), :] = w_ref[...]

    def w_right(step):
        block = wg.at[rows_of(plus(z, -step, NZ)), :]
        return remote(block, block, wr_sem.at[0, step], wr_sem.at[1, step], right)

    def w_left(step):
        block = wg.at[rows_of(plus(z, step, NZ)), :]
        return remote(block, block, wl_sem.at[0, step], wl_sem.at[1, step], left)

    def w_arrived(step):
        if step <= R:
            block = wg.at[rows_of(plus(z, -step, NZ)), :]
            remote(block, block, wr_sem.at[0, step - 1], wr_sem.at[1, step - 1], right).wait_recv()
        if step < R:
            w_right(step).start()
        if step <= L:
            block = wg.at[rows_of(plus(z, step, NZ)), :]
            remote(block, block, wl_sem.at[0, step - 1], wl_sem.at[1, step - 1], left).wait_recv()
        if step < L:
            w_left(step).start()

    w_right(0).start()
    if L > 0:
        w_left(0).start()

    def cot_copy(pair):
        return remote(
            cot_ref,
            cotg.at[rows_of(y), lanes_of(k, OT)],
            cot_s.at[pair[0], pair[1]],
            cot_r.at[y, k],
            dev(x, z, plus(x, pair[0], NX), plus(k, pair[1], NK)),
        )

    for pair in pairs:
        unless_self(pair, lambda: cot_copy(pair).start())

    @pl.when(x == y)
    def _():
        cotg[rows_of(y), lanes_of(k, OT)] = cot_ref[...]

    spread = (lax.div(iota((G, C), 1), MEMBERS) == iota((G, C), 0)).astype(F32)
    rate_ch[...] = jnp.dot(rate_ref[...], spread, precision=HIGHEST, preferred_element_type=F32)
    res_ch = jnp.dot(res_ref[...], spread, precision=HIGHEST, preferred_element_type=F32)
    for i in range(3):
        taps[i, pl.ds(0, TAPS), :] = jnp.dot(
            sf_ref[i], spread, precision=HIGHEST, preferred_element_type=F32
        )
    own_mode = lax.rem(iota((MODES, C), 1), MODES) == iota((MODES, C), 0)
    dec[...] = jnp.exp(-float(ROWS) * rate_ch[...])
    vecs[pl.ds(0, 1), :] = jnp.sum(jnp.where(own_mode, rate_ch[...], 0.0), axis=0, keepdims=True)
    vecs[pl.ds(1, 1), :] = jnp.sum(jnp.where(own_mode, res_ch, 0.0), axis=0, keepdims=True)

    eye = (iota((G, G), 0) == iota((G, G), 1)).astype(F32)
    turned = (((1,), (1,)), ((), ()))
    rate_t = lax.dot_general(eye, rate_ref[...], turned, precision=HIGHEST, preferred_element_type=F32)
    res_t = lax.dot_general(eye, res_ref[...], turned, precision=HIGHEST, preferred_element_type=F32)
    lag = iota((G, LANES), 1).astype(F32)
    ahead = jnp.zeros((G, LANES), F32)
    behind = jnp.zeros((G, LANES), F32)
    for m in range(MODES):
        ahead = ahead + res_t[:, m : m + 1] * jnp.exp(-rate_t[:, m : m + 1] * lag)
        behind = behind + res_t[:, m : m + 1] * jnp.exp(-rate_t[:, m : m + 1] * (ROWS - 1.0 - lag))
    prof[0] = ahead
    prof[1] = behind

    row_id, lane_id = iota((ROWS, LANES), 0), iota((ROWS, LANES), 1)
    lane_group = lax.div(lane_id, MEMBERS)

    def tables(j, carry):
        ls = lanes_of(j)
        rate = vecs[pl.ds(0, 1), ls]
        amp = vecs[pl.ds(1, 1), ls] * jnp.exp(-rate)
        place = row_id.astype(F32)
        early = jnp.exp(-rate * place)
        late = jnp.exp(-rate * (ROWS - 1.0 - place))
        for table, value in ((inf, late), (inb, early)):
            high, low = two_terms(jnp.transpose(value))
            table[j, pl.ds(0, ROWS), :] = high
            table[j, pl.ds(ROWS, ROWS), :] = low
        for table, value in ((entf, amp * early), (entb, amp * late)):
            high, low = two_terms(value)
            table[j, :, pl.ds(0, LANES)] = high
            table[j, :, pl.ds(LANES, LANES)] = low
            table[j, :, pl.ds(2 * LANES, LANES)] = high
        return carry

    def toeplitz(j, carry):
        for g in range(PER_TILE):
            one = prof[0, pl.ds(j * PER_TILE + g, 1), :]
            skew = pltpu.roll(
                jnp.broadcast_to(one, (ROWS, LANES)), 0, 1, stride=1, stride_axis=0
            )
            tb[j, :, pl.ds(g * LANES, LANES)] = jnp.where(lane_id >= row_id, skew, 0.0).astype(BF16)
            one = prof[1, pl.ds(j * PER_TILE + g, 1), :]
            skew = pltpu.roll(
                jnp.broadcast_to(one, (ROWS, LANES)), 1, 1, stride=1, stride_axis=0
            )
            tf[j, :, pl.ds(g * LANES, LANES)] = jnp.where(lane_id <= row_id, skew, 0.0).astype(BF16)
        return carry

    lax.fori_loop(0, NZ, tables, 0)

    for i in range(3):
        xpad[i, pl.ds(8, ROWS), :] = s_ref[i].astype(F32)

    @pl.when(c == 0)
    def _():
        rim_in[...] = jnp.zeros_like(rim_in)

    @pl.when(c > 0)
    def _():
        rim_copy.wait_recv()

    for i in range(3):
        xpad[i, pl.ds(0, 8), :] = rim_in[i].astype(F32)[8:16, :]

    def spread_groups(value):
        return jnp.concatenate(
            [jnp.where(lane_group == g, value, 0.0).astype(BF16) for g in range(PER_TILE)], axis=0
        )

    mode_block = lax.div(row_id, MODES) == lane_group

    def state_of(table, value):
        both = jnp.dot(table, value, preferred_element_type=F32)
        both = jnp.where(mode_block, both[:ROWS] + both[ROWS:], 0.0)
        total = both[:MODES]
        for g in range(1, PER_TILE):
            total = total + both[g * MODES : (g + 1) * MODES]
        return total

    def from_state(table, state):
        tall = jnp.where(mode_block, jnp.concatenate([state] * PER_TILE, axis=0), 0.0)
        high, low = two_terms(tall)
        return jnp.dot(
            table, jnp.concatenate([high, high, low], axis=0), preferred_element_type=F32
        )

    def states_out(way):
        stz[way, z] = st_out[way, z]
        for d in range(1, NZ):
            to = plus(z, d, NZ)
            remote(
                st_out.at[way, to], stz.at[way, z], stz_sem.at[way, 0, d], stz_sem.at[way, 1, d], dev(y, to)
            ).start()

    def states_row(way):
        for d in range(1, NZ):
            src = plus(z, -d, NZ)
            remote(
                st_out.at[way, src], stz.at[way, src], stz_sem.at[way, 0, d], stz_sem.at[way, 1, d], dev(y, src)
            ).wait_recv()
        factor = dec[:, lanes_of(z)]
        state = jnp.zeros((MODES, LANES), F32)
        for i in range(NZ):
            at = i if way == 0 else NZ - 1 - i
            ret_out[way, at] = state
            state = factor * state + stz[way, at]
        tot[way, y] = state
        for d in range(1, NY):
            to = plus(y, d, NY)
            remote(
                tot.at[way, y], tot.at[way, y], tot_sem.at[way, 0, d], tot_sem.at[way, 1, d], dev(to, z)
            ).start()

    def states_back(way):
        for d in range(1, NY):
            src = plus(y, -d, NY)
            remote(
                tot.at[way, src], tot.at[way, src], tot_sem.at[way, 0, d], tot_sem.at[way, 1, d], dev(src, z)
            ).wait_recv()
        factor = dec[:, lanes_of(z)]
        row_factor = jnp.exp(-float(ROWS * NZ) * rate_ch[:, lanes_of(z)])
        state = jnp.zeros((MODES, LANES), F32)
        for i in range(NY):
            at = i if way == 0 else NY - 1 - i
            counts = (at < y) if way == 0 else (at > y)
            state = jnp.where(counts, row_factor * state + tot[way, at], state)
        for i in range(NZ):
            at = i if way == 0 else NZ - 1 - i
            ret_out[way, at] = ret_out[way, at] + state
            state = state * factor
        bef[way, z] = ret_out[way, z]
        for d in range(1, NZ):
            to = plus(z, d, NZ)
            remote(
                ret_out.at[way, to], bef.at[way, z], bef_sem.at[way, 0, d], bef_sem.at[way, 1, d], dev(y, to)
            ).start()

    def states_in(way):
        for d in range(1, NZ):
            src = plus(z, -d, NZ)
            remote(
                ret_out.at[way, src], bef.at[way, src], bef_sem.at[way, 0, d], bef_sem.at[way, 1, d], dev(y, src)
            ).wait_recv()

    def smooth(j, carry):
        ls = lanes_of(j)
        for i in range(3):
            total = taps[i, pl.ds(0, 1), ls] * xpad[i, pl.ds(8, ROWS), ls]
            for n in range(1, TAPS):
                total = total + taps[i, pl.ds(n, 1), ls] * xpad[i, pl.ds(8 - n, ROWS), ls]
            sm[i, :, ls] = total
        value = (sm[1, :, ls] * sm[2, :, ls]).astype(BF16)
        mixed[:, ls] = value
        st_out[0, j] = state_of(inf[j], value)
        return carry

    lax.fori_loop(0, NZ, smooth, 0)
    states_out(0)
    if NZ > 1:
        w_arrived(1)
    lax.fori_loop(0, NZ, toeplitz, 0)

    def local_field(j, carry):
        ls = lanes_of(j)
        value = mixed[:, ls].astype(F32)
        field[:, ls] = skip_ref[:, ls] * value + jnp.dot(
            tf[j], spread_groups(value), preferred_element_type=F32
        )
        return carry

    states_row(0)
    lax.fori_loop(0, NZ, local_field, 0)
    states_back(0)
    if R >= 2:
        w_arrived(2)
    states_in(0)

    def gate(j, carry):
        ls = lanes_of(j)
        value = field[:, ls] + from_state(entf[j], bef[0, j])
        field[:, ls] = value
        gg[rows_of(y), ls] = (sm[0, :, ls] * value).astype(BF16)
        return carry

    lax.fori_loop(0, NZ, gate, 0)

    def g_copy(d):
        return remote(
            gg.at[rows_of(y), :], gg.at[rows_of(y), :], g_sem.at[0, d], g_sem.at[1, d], dev(plus(y, d, NY), z)
        )

    for d in range(1, NY):
        g_copy(d).start()

    for step in range(3, R + 1):
        w_arrived(step)
    for a in range(NY):
        for b in range(NK):

            def cot_wait():
                block = cotg.at[pl.ds(a * ROWS, ROWS), pl.ds(b * OT, OT)]
                remote(block, block, cot_s.at[0, 0], cot_r.at[a, b], dev(y, z)).wait_recv()

            pl.when(jnp.logical_not((x == y) & (y == a) & (k == b)))(cot_wait)

    WIDE = 256

    def up_part(j, carry):
        ls = lanes_of(j, WIDE)
        upp[:, ls] = jnp.dot(cotg[...], wg[:, ls], preferred_element_type=F32).astype(BF16)
        return carry

    lax.fori_loop(0, C // WIDE, up_part, 0)

    def up_copy(d):
        to = plus(y, d, NY)
        return remote(upp.at[rows_of(to), :], up_in.at[d], up_sem.at[0, d], up_sem.at[1, d], dev(to, z))

    for d in range(1, NY):
        up_copy(d).start()

    for d in range(1, NY):
        src = plus(y, -d, NY)
        block = gg.at[rows_of(src), :]
        remote(block, block, g_sem.at[0, d], g_sem.at[1, d], dev(src, z)).wait_recv()

    over_rows = (((0,), (0,)), ((), ()))

    def gw_part(i, carry):
        block = lax.rem(z + R + NZ - i, NZ)
        gwp[block] = lax.dot_general(
            cotg[:, lanes_of(block)], gg[...], over_rows, preferred_element_type=F32
        ).astype(BF16)
        return carry

    def gw_right(step):
        return remote(
            gwp.at[plus(z, R - step, NZ)], gw_r.at[step], gwr_sem.at[0, step], gwr_sem.at[1, step], right
        )

    def gw_left(step):
        return remote(
            gwp.at[plus(z, step - L, NZ)], gw_l.at[step], gwl_sem.at[0, step], gwl_sem.at[1, step], left
        )

    def gw_arrived(step):
        if step <= R:
            gw_right(step - 1).wait_recv()
        if step < R:
            at = plus(z, R - step, NZ)
            gwp[at] = (gwp[at].astype(F32) + gw_r[step - 1].astype(F32)).astype(BF16)
            gw_right(step).start()
        if step <= L:
            gw_left(step - 1).wait_recv()
        if step < L:
            at = plus(z, step - L, NZ)
            gwp[at] = (gwp[at].astype(F32) + gw_l[step - 1].astype(F32)).astype(BF16)
            gw_left(step).start()

    lax.fori_loop(0, NZ, gw_part, 0)
    gw_right(0).start()
    if L > 0:
        gw_left(0).start()

    def out_part(j, carry):
        ls = lanes_of(j, WIDE)
        outp[:, ls] = lax.dot_general(gg[...], wg[ls, :], turned, preferred_element_type=F32).astype(BF16)
        return carry

    lax.fori_loop(0, OY // WIDE, out_part, 0)

    def out_copy(pair):
        yy, kk = plus(y, pair[0], NY), plus(k, pair[1], NK)
        return remote(
            outp.at[rows_of(yy), lanes_of(kk, OT)],
            out_in.at[p],
            out_s.at[pair[0], pair[1]],
            out_r.at[x, k],
            dev(yy, z, y, kk),
        )

    for pair in pairs:
        unless_self(pair, lambda: out_copy(pair).start())

    @pl.when(x == y)
    def _():
        out_in[p] = outp[rows_of(y), lanes_of(k, OT)]

    for d in range(1, NY):
        up_copy(d).wait_recv()

    def grad_field(j, carry):
        ls = lanes_of(j)
        up = upp[rows_of(y), ls].astype(F32)
        for d in range(1, NY):
            up = up + up_in[d, :, ls].astype(F32)
        gf = up * sm[0, :, ls]
        gsp[0, pl.ds(0, ROWS), ls] = up * field[:, ls]
        gm[:, ls] = skip_ref[:, ls] * gf
        sml[pl.ds(24 + j, 1), :] = jnp.sum(gf * mixed[:, ls].astype(F32), axis=0, keepdims=True)
        value = gf.astype(BF16)
        gfb[:, ls] = value
        st_out[1, j] = state_of(inb[j], value)
        return carry

    lax.fori_loop(0, NZ, grad_field, 0)
    states_out(1)

    def local_grad(j, carry):
        ls = lanes_of(j)
        gm[:, ls] = gm[:, ls] + jnp.dot(
            tb[j], spread_groups(gfb[:, ls].astype(F32)), preferred_element_type=F32
        )
        return carry

    def tap_grad(i, j):
        ls = lanes_of(j)
        value = gsp[i, pl.ds(0, ROWS), ls]
        for n in range(TAPS):
            tapsum[pl.ds(i * TAPS + n, 1), ls] = jnp.sum(
                value * xpad[i, pl.ds(8 - n, ROWS), ls], axis=0, keepdims=True
            )

    lax.fori_loop(0, NZ, local_grad, 0)
    states_row(1)
    gw_arrived(1)

    def first_taps(j, carry):
        tap_grad(0, j)
        return carry

    states_back(1)
    lax.fori_loop(0, NZ, first_taps, 0)
    states_in(1)

    def grad_mixed(j, carry):
        ls = lanes_of(j)
        value = gm[:, ls] + from_state(entb[j], bef[1, j])
        gsp[1, pl.ds(0, ROWS), ls] = value * sm[2, :, ls]
        gsp[2, pl.ds(0, ROWS), ls] = value * sm[1, :, ls]
        return carry

    lax.fori_loop(0, NZ, grad_mixed, 0)

    grim_copy = remote(
        gsp.at[:, pl.ds(0, 8), :],
        gsp.at[:, pl.ds(ROWS, 8), :],
        grim_sem.at[0],
        grim_sem.at[1],
        (lax.rem(c + last, last + 1), p),
    )

    @pl.when(c > 0)
    def _():
        grim_copy.start()

    if R >= 2:
        gw_arrived(2)

    def other_taps(j, carry):
        tap_grad(1, j)
        tap_grad(2, j)
        return carry

    lax.fori_loop(0, NZ, other_taps, 0)
    tapsum[pl.ds(3 * TAPS, 3), :] = jnp.zeros((3, C), F32)
    gather_groups = (lax.div(iota((C, LANES), 0), MEMBERS) == iota((C, LANES), 1)).astype(F32)
    sml[pl.ds(0, 24), :] = jnp.dot(
        tapsum[...], gather_groups, precision=HIGHEST, preferred_element_type=F32
    )

    def small_z(d):
        return remote(sml, smz.at[d], smz_sem.at[0, d], smz_sem.at[1, d], dev(y, plus(z, d, NZ)))

    def small_y(d):
        return remote(smy.at[0], smy.at[d], smy_sem.at[0, d], smy_sem.at[1, d], dev(plus(y, d, NY), z))

    for d in range(1, NZ):
        small_z(d).start()

    @pl.when(c == last)
    def _():
        gsp[:, pl.ds(ROWS, 8), :] = jnp.zeros((3, 8, C), F32)

    @pl.when(c < last)
    def _():
        grim_copy.wait_recv()

    def streams_grad(j, carry):
        ls = lanes_of(j)
        for i in range(3):
            total = taps[i, pl.ds(0, 1), ls] * gsp[i, pl.ds(0, ROWS), ls]
            for n in range(1, TAPS):
                total = total + taps[i, pl.ds(n, 1), ls] * gsp[i, pl.ds(n, ROWS), ls]
            gs_ref[i, :, ls] = total.astype(BF16)
        return carry

    lax.fori_loop(0, NZ, streams_grad, 0)

    total = sml[...]
    for d in range(1, NZ):
        small_z(d).wait_recv()
        total = total + smz[d]
    smy[0] = total
    for d in range(1, NY):
        small_y(d).start()

    for step in range(3, R + 1):
        gw_arrived(step)
    mine = gwp[z].astype(F32) + gw_r[R - 1].astype(F32)
    if L > 0:
        mine = mine + gw_l[L - 1].astype(F32)
    gw_ref[...] = mine

    for a in range(NX):
        for b in range(NK):

            def out_wait():
                block = out_in.at[a * NK + b]
                remote(block, block, out_s.at[0, 0], out_r.at[a, b], dev(y, z)).wait_recv()

            pl.when(jnp.logical_not((x == y) & (x == a) & (k == b)))(out_wait)
    value = out_in[0].astype(F32)
    for n in range(1, NX * NK):
        value = value + out_in[n].astype(F32)
    out_ref[...] = value.astype(BF16)

    total = smy[0]
    for d in range(1, NY):
        small_y(d).wait_recv()
        total = total + smy[d]
    for i in range(3):
        gshort_ref[i] = total[i * TAPS : (i + 1) * TAPS, :G]
    for j in range(NZ):
        gskip_ref[:, pl.ds(j * LANES, LANES)] = total[24 + j : 25 + j, :]

    @pl.when(c < last)
    def _():
        rim_copy.wait_send()

    @pl.when(c > 0)
    def _():
        grim_copy.wait_send()

    for step in range(R):
        w_right(step).wait_send()
        gw_right(step).wait_send()
    for step in range(L):
        w_left(step).wait_send()
        gw_left(step).wait_send()
    for pair in pairs:
        unless_self(pair, lambda: cot_copy(pair).wait_send())
        unless_self(pair, lambda: out_copy(pair).wait_send())
    for d in range(1, NY):
        g_copy(d).wait_send()
        up_copy(d).wait_send()
        small_y(d).wait_send()
        for way in range(2):
            remote(tot.at[way, y], tot.at[way, y], tot_sem.at[way, 0, d], tot_sem.at[way, 1, d], right).wait_send()
    for d in range(1, NZ):
        small_z(d).wait_send()
        for way in range(2):
            for buf, sem in ((st_out, stz_sem), (ret_out, bef_sem)):
                block = buf.at[way, plus(z, d, NZ)]
                remote(block, block, sem.at[way, 0, d], sem.at[way, 1, d], right).wait_send()


def shards(dims, streams, short_filter, residues, rates, skip, out_weight, out_cotangent):
    NX, NY, NZ, NK = dims
    C = streams.shape[2]
    G = residues.shape[1]
    OT = out_cotangent.shape[1]
    OY = NZ * ROWS
    R = NZ // 2
    L = max(NZ - 1 - R, 1)
    vmem = pltpu.VMEM
    dma = pltpu.SemaphoreType.DMA
    whole = pl.BlockSpec(memory_space=pltpu.VMEM)
    scratch = [
        vmem((3, ROWS + 8, C), F32),
        vmem((3, 16, C), BF16),
        vmem((3, ROWS, C), F32),
        vmem((ROWS, C), BF16),
        vmem((ROWS, C), F32),
        vmem((ROWS, C), BF16),
        vmem((ROWS, C), F32),
        vmem((NZ, ROWS, PER_TILE * LANES), BF16),
        vmem((NZ, ROWS, PER_TILE * LANES), BF16),
        vmem((NZ, 2 * ROWS, LANES), BF16),
        vmem((NZ, 2 * ROWS, LANES), BF16),
        vmem((NZ, ROWS, 3 * LANES), BF16),
        vmem((NZ, ROWS, 3 * LANES), BF16),
        vmem((MODES, C), F32),
        vmem((MODES, C), F32),
        vmem((8, C), F32),
        vmem((3, 8, C), F32),
        vmem((2, G, LANES), F32),
        vmem((2, NZ, MODES, LANES), F32),
        vmem((2, NZ, MODES, LANES), F32),
        vmem((2, NY, MODES, LANES), F32),
        vmem((2, NZ, MODES, LANES), F32),
        vmem((2, NZ, MODES, LANES), F32),
        vmem((OY, C), BF16),
        vmem((NY * ROWS, OY), BF16),
        vmem((NY * ROWS, C), BF16),
        vmem((NY * ROWS, C), BF16),
        vmem((NY, ROWS, C), BF16),
        vmem((NY * ROWS, OY), BF16),
        vmem((NX * NK, ROWS, OT), BF16),
        vmem((NZ, ROWS, C), BF16),
        vmem((R, ROWS, C), BF16),
        vmem((L, ROWS, C), BF16),
        vmem((3, ROWS + 8, C), F32),
        vmem((24, C), F32),
        vmem((32, LANES), F32),
        vmem((NZ, 32, LANES), F32),
        vmem((NY, 32, LANES), F32),
        dma((2,)),
        dma((NX, NK)),
        dma((NY, NK)),
        dma((2, R)),
        dma((2, L)),
        dma((2, 2, NZ)),
        dma((2, 2, NY)),
        dma((2, 2, NZ)),
        dma((2, NY)),
        dma((2, NY)),
        dma((NY, NK)),
        dma((NX, NK)),
        dma((2, R)),
        dma((2, L)),
        dma((2,)),
        dma((2, NZ)),
        dma((2, NY)),
    ]
    output, grad_streams, grad_short, grad_skip, grad_weight = pl.pallas_call(
        functools.partial(kernel, dims),
        out_shape=(
            jax.ShapeDtypeStruct((ROWS, OT), BF16),
            jax.ShapeDtypeStruct(streams.shape, BF16),
            jax.ShapeDtypeStruct(short_filter.shape, F32),
            jax.ShapeDtypeStruct((1, C), F32),
            jax.ShapeDtypeStruct((ROWS, C), F32),
        ),
        in_specs=[whole] * 7,
        out_specs=(whole,) * 5,
        scratch_shapes=scratch,
        compiler_params=pltpu.CompilerParams(
            collective_id=0, has_side_effects=True, vmem_limit_bytes=56 * 1024 * 1024
        ),
        name="mixer",
    )(streams, short_filter, residues, rates, skip.reshape(1, C), out_weight, out_cotangent)
    return output, grad_streams, grad_short, grad_skip.reshape(C), grad_weight


def build(mesh, dims):
    return jax.shard_map(
        functools.partial(shards, dims),
        mesh=mesh,
        in_specs=(
            P(None, "ctx", "tp"),
            P(None, None, "tp"),
            P(None, "tp"),
            P(None, "tp"),
            P("tp"),
            P("ctx", "tp"),
            P("ctx", "tp"),
        ),
        out_specs=(
            P("ctx", "tp"),
            P(None, "ctx", "tp"),
            P(None, None, "tp"),
            P("tp"),
            P("ctx", "tp"),
        ),
        check_vma=False,
    )


def solution(mesh):
    return build(mesh, (4, 4, 8, 2))
```

time: 600 us -> 136 us (0.23); the launches traced: 593 us -> 136 us
  blocking collectives: 194 us -> 0 us
  waiting for transfers between devices: 176 us -> 0 us
  Pallas kernels: 0 us -> 130 us
  local copies, waits for them, and re-layouts: 119 us -> 5.76 us
  matrix products: 43.5 us -> 0 us
  other arithmetic: 38 us -> 0 us
  between operations: 14.8 us -> 0.65 us
    psum x1 -> x0, blocking collectives: 141 us -> none  [shards(): grad_skip, grad_short = lax.psum((skip_part, tap_part), 'ctx')]
    pallas_call x0 -> x1, Pallas kernels: none -> 130 us  [shards(): pl.pallas_call(functools.partial(kernel, dims), out_shape=(jax.ShapeDtype...]
    all_gather x4 -> x0, waiting for transfers between devices: 126 us -> none  [the longest x1 81.9 us: shards(): weights = lax.all_gather(out_weight, 'ctx', axis=0, tiled=True)]
    gather x2 -> x0, local copies, waits for them, and re-layouts: 61.9 us -> none  [modal_tables(): jnp.take(profile, jnp.maximum(offset, 0), axis=0)]
    all_gather x1 -> x0, blocking collectives: 53.3 us -> none  [entering_2(): gathered = jax.tree.map(lambda a: lax.all_gather(a, axis), part)]
    dot_general x10 -> x0, matrix products: 43.5 us -> none  [the longest x2 15.4 us: local_pass(): local = jnp.einsum('tsg,sgc->tgc', toeplitz, source, precision=highest)]
    add x33 -> x0, other arithmetic: 31.2 us -> none  [the longest x31 29.7 us: combine(): return (earlier[0] * later[0], later[0][:, :, None] * earlier[1] + later[1])]
    reduce_scatter x1 -> x0, waiting for transfers between devices: 29 us -> none  [shards(): lax.psum_scatter(partial_value.astype(jnp.bfloat16), 'tp', scatter_dimens...]
  transfers between devices with their start and end apart: 8 -> 0, of which waited for: 4 -> 0; matrix products, arithmetic and copies ran while one was open for 30% -> 0% of each run, Pallas kernels for 0% -> 0%
where the time goes in v1:
time: 136 us
  Pallas kernels  130 us (96%)
  local copies, waits for them, and re-layouts  5.76 us (4%)
    pallas_call x1, Pallas kernels, shards(): pl.pallas_call(functools.partial(kernel, dims), out_shape=(jax.ShapeDtype...  130 us
    unnamed x11, local copies, waits for them, and re-layouts  5.76 us

profile of v1, /device:TPU:4, one launch (start us, length us, event | category | flops | bytes accessed | tf_op | source)
XLA Modules:
  0.0 136.1 jit_solution(214916958158004019)
XLA Ops:
  0.6 129.7 %mixer.1 = (bf16[128,512]{1,0:T(8,128)(2,1)}, bf16[3,128,1024]{2,1,0:T(8,128)(2,1)}, f32[3,7,64]{2,1,0:T(8,128)}, f32[1,1024]{1,0:T(1,128)}, f32[128,1024]{1,0:T(8,128)}) custom-call(bf16[3,128,1024]{2,1,0:T(8,128)(2,1)} %s_ref.1, f32[3,7,64]{2,1,0:T(8,128)} %sf_ref.1, f32[16,64]{1,0:T(8,128)} %res_ref.1, f32[16,64]{1,0:T(8,128)} %rate_ref.1, ...), custom_call_target="tpu_custom_call" | custom-call | tf_op jit(solution)/shard_map/mixer/pallas_call | solution.py:762
  130.3 1.6 %copy.17 = bf16[128,512]{1,0:T(8,128)(2,1)} copy(bf16[128,512]{1,0:T(8,128)(2,1)} %get-tuple-element.20) | data formatting | bytes 262144
  131.9 0.0 copy-start.1
  131.9 0.0 copy-start
  131.9 2.1 %copy.18 = bf16[3,128,1024]{2,1,0:T(8,128)(2,1)} copy(bf16[3,128,1024]{2,1,0:T(8,128)(2,1)} %get-tuple-element.21) | data formatting | bytes 1572864
  134.0 0.0 copy-done.1
  134.0 0.0 copy-start.2
  134.0 0.6 copy.19
  134.6 0.1 copy-done.2
  134.7 0.6 copy.20
  135.3 0.0 copy-done
  135.3 0.8 copy.21
Async XLA Ops:
  131.9 2.1 %copy-start.1 = (f32[3,7,64]{2,1,0:T(8,128)S(1)}, f32[3,7,64]{2,1,0:T(8,128)}, u32[]{:S(2)}) copy-start(f32[3,7,64]{2,1,0:T(8,128)} %get-tuple-element.22) | copy-start | bytes 16132
  131.9 3.4 %copy-start = (f32[128,1024]{1,0:T(8,128)S(1)}, f32[128,1024]{1,0:T(8,128)}, u32[]{:S(2)}) copy-start(f32[128,1024]{1,0:T(8,128)} %get-tuple-element.24) | copy-start | bytes 1572868
  134.0 0.7 copy-start.2

commit v2 on v1

--- a/solution.py
+++ b/solution.py
@@ -12,6 +12,7 @@
 HIGHEST = lax.Precision.HIGHEST
 MESH = pl.DeviceIdType.MESH
 ROWS = 128
+HALF = 64
 LANES = 128
 MEMBERS = 16
 MODES = 16
@@ -71,7 +72,10 @@
     upp,
     up_in,
     outp,
-    out_in,
+    pair_in,
+    outh,
+    out_y,
+    out_x,
     gwp,
     gw_r,
     gw_l,
@@ -90,8 +94,9 @@
     bef_sem,
     g_sem,
     up_sem,
-    out_s,
-    out_r,
+    pair_sem,
+    outy_sem,
+    outx_sem,
     gwr_sem,
     gwl_sem,
     grim_sem,
@@ -104,7 +109,6 @@
     OT = cot_ref.shape[1]
     OY = NZ * ROWS
     R = NZ // 2
-    L = NZ - 1 - R
     c = lax.axis_index("ctx")
     p = lax.axis_index("tp")
     y, z = lax.div(c, NZ), lax.rem(c, NZ)
@@ -145,6 +149,10 @@
         greet(dev(y, plus(z, d, NZ)))
     for d in range(1, NY):
         greet(dev(plus(y, d, NY), z))
+    for d in range(1, NX):
+        greet(dev(y, z, plus(x, d, NX)))
+    for d in range(1, NK):
+        greet(dev(y, z, x, plus(k, d, NK)))
     for pair in pairs:
         unless_self(pair, lambda: greet(dev(x, z, plus(x, pair[0], NX), plus(k, pair[1], NK))))
         unless_self(pair, lambda: greet(dev(plus(y, pair[0], NY), z, y, plus(k, pair[1], NK))))
@@ -156,61 +164,6 @@
     @pl.when(c < last)
     def _():
         greet((c + 1, p))
-
-    peers = NZ - 1 + NY - 1 + 2 * (NX * NK - 1)
-    peers = peers + jnp.where(x != y, 2, 0) + jnp.where(c > 0, 1, 0) + jnp.where(c < last, 1, 0)
-    pl.semaphore_wait(barrier, peers)
-
-    rim_copy = remote(
-        s_ref.at[:, pl.ds(ROWS - 16, 16), :], rim_in, rim_sem.at[0], rim_sem.at[1], (lax.rem(c + 1, last + 1), p)
-    )
-
-    @pl.when(c < last)
-    def _():
-        rim_copy.start()
-
-    right, left = dev(y, plus(z, 1, NZ)), dev(y, plus(z, -1, NZ))
-    wg[rows_of(z), :] = w_ref[...]
-
-    def w_right(step):
-        block = wg.at[rows_of(plus(z, -step, NZ)), :]
-        return remote(block, block, wr_sem.at[0, step], wr_sem.at[1, step], right)
-
-    def w_left(step):
-        block = wg.at[rows_of(plus(z, step, NZ)), :]
-        return remote(block, block, wl_sem.at[0, step], wl_sem.at[1, step], left)
-
-    def w_arrived(step):
-        if step <= R:
-            block = wg.at[rows_of(plus(z, -step, NZ)), :]
-            remote(block, block, wr_sem.at[0, step - 1], wr_sem.at[1, step - 1], right).wait_recv()
-        if step < R:
-            w_right(step).start()
-        if step <= L:
-            block = wg.at[rows_of(plus(z, step, NZ)), :]
-            remote(block, block, wl_sem.at[0, step - 1], wl_sem.at[1, step - 1], left).wait_recv()
-        if step < L:
-            w_left(step).start()
-
-    w_right(0).start()
-    if L > 0:
-        w_left(0).start()
-
-    def cot_copy(pair):
-        return remote(
-            cot_ref,
-            cotg.at[rows_of(y), lanes_of(k, OT)],
-            cot_s.at[pair[0], pair[1]],
-            cot_r.at[y, k],
-            dev(x, z, plus(x, pair[0], NX), plus(k, pair[1], NK)),
-        )
-
-    for pair in pairs:
-        unless_self(pair, lambda: cot_copy(pair).start())
-
-    @pl.when(x == y)
-    def _():
-        cotg[rows_of(y), lanes_of(k, OT)] = cot_ref[...]
 
     spread = (lax.div(iota((G, C), 1), MEMBERS) == iota((G, C), 0)).astype(F32)
     rate_ch[...] = jnp.dot(rate_ref[...], spread, precision=HIGHEST, preferred_element_type=F32)
@@ -276,6 +229,67 @@
 
     for i in range(3):
         xpad[i, pl.ds(8, ROWS), :] = s_ref[i].astype(F32)
+
+    peers = NZ - 1 + NY - 1 + NX - 1 + NK - 1 + 2 * (NX * NK - 1)
+    peers = peers + jnp.where(x != y, 2, 0) + jnp.where(c > 0, 1, 0) + jnp.where(c < last, 1, 0)
+    pl.semaphore_wait(barrier, peers)
+
+    rim_copy = remote(
+        s_ref.at[:, pl.ds(ROWS - 16, 16), :], rim_in, rim_sem.at[0], rim_sem.at[1], (lax.rem(c + 1, last + 1), p)
+    )
+
+    @pl.when(c < last)
+    def _():
+        rim_copy.start()
+
+    right, left = dev(y, plus(z, 1, NZ)), dev(y, plus(z, -1, NZ))
+    wg[rows_of(z), :] = w_ref[...]
+
+    def long_way(direction, half):
+        return R if direction == half else R - 1
+
+    def half_rows(block, half):
+        return pl.ds(pl.multiple_of(block * ROWS + half * HALF, HALF), HALF)
+
+    def w_copy(direction, half, step):
+        sem = wr_sem if direction == 0 else wl_sem
+        block = wg.at[half_rows(plus(z, -step if direction == 0 else step, NZ), half), :]
+        return remote(block, block, sem.at[0, half, step], sem.at[1, half, step], right if direction == 0 else left)
+
+    def w_arrived(step, lap):
+        for direction in range(2):
+            half = direction if lap == 0 else 1 - direction
+            steps = long_way(direction, half)
+            if step <= steps:
+                sem = wr_sem if direction == 0 else wl_sem
+                block = wg.at[half_rows(plus(z, -step if direction == 0 else step, NZ), half), :]
+                remote(block, block, sem.at[0, half, step - 1], sem.at[1, half, step - 1], right).wait_recv()
+            if step < steps:
+                w_copy(direction, half, step).start()
+
+    for lap in range(2):
+        for direction in range(2):
+            half = direction if lap == 0 else 1 - direction
+            if long_way(direction, half) > 0:
+                w_copy(direction, half, 0).start()
+
+    def cot_copy(pair):
+        return remote(
+            cot_ref,
+            cotg.at[rows_of(y), lanes_of(k, OT)],
+            cot_s.at[pair[0], pair[1]],
+            cot_r.at[y, k],
+            dev(x, z, plus(x, pair[0], NX), plus(k, pair[1], NK)),
+        )
+
+    for pair in pairs:
+        unless_self(pair, lambda: cot_copy(pair).start())
+
+    @pl.when(x == y)
+    def _():
+        cotg[rows_of(y), lanes_of(k, OT)] = cot_ref[...]
+
+    lax.fori_loop(0, NZ, toeplitz, 0)
 
     @pl.when(c == 0)
     def _():
@@ -382,9 +396,7 @@
 
     lax.fori_loop(0, NZ, smooth, 0)
     states_out(0)
-    if NZ > 1:
-        w_arrived(1)
-    lax.fori_loop(0, NZ, toeplitz, 0)
+    w_arrived(1, 0)
 
     def local_field(j, carry):
         ls = lanes_of(j)
@@ -394,11 +406,17 @@
         )
         return carry
 
+    lax.fori_loop(0, R, local_field, 0)
+    w_arrived(1, 1)
+    lax.fori_loop(R, NZ, local_field, 0)
+    for step, lap in [(2, 0)]:
+        w_arrived(step, lap)
     states_row(0)
-    lax.fori_loop(0, NZ, local_field, 0)
+    for step, lap in [(2, 1), (3, 0)]:
+        w_arrived(step, lap)
     states_back(0)
-    if R >= 2:
-        w_arrived(2)
+    for step, lap in [(3, 1)] + [(n, lap) for n in range(4, R + 1) for lap in range(2)]:
+        w_arrived(step, lap)
     states_in(0)
 
     def gate(j, carry):
@@ -418,8 +436,6 @@
     for d in range(1, NY):
         g_copy(d).start()
 
-    for step in range(3, R + 1):
-        w_arrived(step)
     for a in range(NY):
         for b in range(NK):
 
@@ -459,34 +475,39 @@
         ).astype(BF16)
         return carry
 
-    def gw_right(step):
+    def gw_block(direction, half, step):
+        far = long_way(direction, half) - step
+        return plus(z, far if direction == 0 else -far, NZ)
+
+    def gw_copy(direction, half, step):
+        sem, into = (gwr_sem, gw_r) if direction == 0 else (gwl_sem, gw_l)
         return remote(
-            gwp.at[plus(z, R - step, NZ)], gw_r.at[step], gwr_sem.at[0, step], gwr_sem.at[1, step], right
-        )
-
-    def gw_left(step):
-        return remote(
-            gwp.at[plus(z, step - L, NZ)], gw_l.at[step], gwl_sem.at[0, step], gwl_sem.at[1, step], left
-        )
-
-    def gw_arrived(step):
-        if step <= R:
-            gw_right(step - 1).wait_recv()
-        if step < R:
-            at = plus(z, R - step, NZ)
-            gwp[at] = (gwp[at].astype(F32) + gw_r[step - 1].astype(F32)).astype(BF16)
-            gw_right(step).start()
-        if step <= L:
-            gw_left(step - 1).wait_recv()
-        if step < L:
-            at = plus(z, step - L, NZ)
-            gwp[at] = (gwp[at].astype(F32) + gw_l[step - 1].astype(F32)).astype(BF16)
-            gw_left(step).start()
+            gwp.at[gw_block(direction, half, step), pl.ds(half * HALF, HALF), :],
+            into.at[half, step],
+            sem.at[0, half, step],
+            sem.at[1, half, step],
+            right if direction == 0 else left,
+        )
+
+    def gw_arrived(step, lap):
+        for direction in range(2):
+            half = direction if lap == 0 else 1 - direction
+            steps = long_way(direction, half)
+            if step <= steps:
+                gw_copy(direction, half, step - 1).wait_recv()
+            if step < steps:
+                at = gw_block(direction, half, step)
+                came = gw_r if direction == 0 else gw_l
+                rows = pl.ds(half * HALF, HALF)
+                gwp[at, rows, :] = (gwp[at, rows, :].astype(F32) + came[half, step - 1].astype(F32)).astype(BF16)
+                gw_copy(direction, half, step).start()
 
     lax.fori_loop(0, NZ, gw_part, 0)
-    gw_right(0).start()
-    if L > 0:
-        gw_left(0).start()
+    for lap in range(2):
+        for direction in range(2):
+            half = direction if lap == 0 else 1 - direction
+            if long_way(direction, half) > 0:
+                gw_copy(direction, half, 0).start()
 
     def out_part(j, carry):
         ls = lanes_of(j, WIDE)
@@ -495,22 +516,52 @@
 
     lax.fori_loop(0, OY // WIDE, out_part, 0)
 
-    def out_copy(pair):
-        yy, kk = plus(y, pair[0], NY), plus(k, pair[1], NK)
+    def pair_copy():
         return remote(
-            outp.at[rows_of(yy), lanes_of(kk, OT)],
-            out_in.at[p],
-            out_s.at[pair[0], pair[1]],
-            out_r.at[x, k],
-            dev(yy, z, y, kk),
-        )
-
-    for pair in pairs:
-        unless_self(pair, lambda: out_copy(pair).start())
-
-    @pl.when(x == y)
-    def _():
-        out_in[p] = outp[rows_of(y), lanes_of(k, OT)]
+            outp.at[:, lanes_of(1 - k, OT)], pair_in, pair_sem.at[0], pair_sem.at[1], dev(y, z, x, 1 - k)
+        )
+
+    def outy_copy(d):
+        to = plus(y, d, NY)
+        return remote(outh.at[rows_of(to), :], out_y.at[y], outy_sem.at[0, d], outy_sem.at[1, d], dev(to, z))
+
+    def outx_copy(d):
+        to = plus(x, d, NX)
+        return remote(out_y.at[to], out_x.at[x], outx_sem.at[0, d], outx_sem.at[1, d], dev(y, z, to))
+
+    if NK == 2:
+        pair_copy().start()
+
+    def out_over_y():
+        if NK == 2:
+            pair_copy().wait_recv()
+            outh[...] = (outp[:, lanes_of(k, OT)].astype(F32) + pair_in[...].astype(F32)).astype(BF16)
+        else:
+            outh[...] = outp[...]
+        for d in range(1, NY):
+            outy_copy(d).start()
+        out_y[y] = outh[rows_of(y), :]
+
+    def out_over_x():
+        for d in range(1, NY):
+            block = out_y.at[plus(y, -d, NY)]
+            remote(block, block, outy_sem.at[0, d], outy_sem.at[1, d], right).wait_recv()
+        for d in range(1, NX):
+            outx_copy(d).start()
+        out_x[x] = out_y[x]
+
+    def out_done():
+        for d in range(1, NX):
+            block = out_x.at[plus(x, -d, NX)]
+            remote(block, block, outx_sem.at[0, d], outx_sem.at[1, d], right).wait_recv()
+        value = out_x[0].astype(F32)
+        for n in range(1, NX):
+            value = value + out_x[n].astype(F32)
+        out_ref[...] = value.astype(BF16)
+
+    gw_arrived(1, 0)
+    out_over_y()
+    gw_arrived(1, 1)
 
     for d in range(1, NY):
         up_copy(d).wait_recv()
@@ -547,16 +598,31 @@
                 value * xpad[i, pl.ds(8 - n, ROWS), ls], axis=0, keepdims=True
             )
 
+    gw_arrived(2, 0)
     lax.fori_loop(0, NZ, local_grad, 0)
+    gw_arrived(2, 1)
+    out_over_x()
     states_row(1)
-    gw_arrived(1)
+    gw_arrived(3, 0)
 
     def first_taps(j, carry):
         tap_grad(0, j)
         return carry
 
+    lax.fori_loop(0, NZ, first_taps, 0)
     states_back(1)
-    lax.fori_loop(0, NZ, first_taps, 0)
+    gw_arrived(3, 1)
+    out_done()
+    for n in range(4, R + 1):
+        for lap in range(2):
+            gw_arrived(n, lap)
+    for half in range(2):
+        rows = pl.ds(half * HALF, HALF)
+        mine = gwp[z, rows, :].astype(F32)
+        for direction, came in ((0, gw_r), (1, gw_l)):
+            if long_way(direction, half) > 0:
+                mine = mine + came[half, long_way(direction, half) - 1].astype(F32)
+        gw_ref[rows, :] = mine
     states_in(1)
 
     def grad_mixed(j, carry):
@@ -580,9 +646,6 @@
     def _():
         grim_copy.start()
 
-    if R >= 2:
-        gw_arrived(2)
-
     def other_taps(j, carry):
         tap_grad(1, j)
         tap_grad(2, j)
@@ -630,26 +693,6 @@
     smy[0] = total
     for d in range(1, NY):
         small_y(d).start()
-
-    for step in range(3, R + 1):
-        gw_arrived(step)
-    mine = gwp[z].astype(F32) + gw_r[R - 1].astype(F32)
-    if L > 0:
-        mine = mine + gw_l[L - 1].astype(F32)
-    gw_ref[...] = mine
-
-    for a in range(NX):
-        for b in range(NK):
-
-            def out_wait():
-                block = out_in.at[a * NK + b]
-                remote(block, block, out_s.at[0, 0], out_r.at[a, b], dev(y, z)).wait_recv()
-
-            pl.when(jnp.logical_not((x == y) & (x == a) & (k == b)))(out_wait)
-    value = out_in[0].astype(F32)
-    for n in range(1, NX * NK):
-        value = value + out_in[n].astype(F32)
-    out_ref[...] = value.astype(BF16)
 
     total = smy[0]
     for d in range(1, NY):
@@ -668,15 +711,19 @@
     def _():
         grim_copy.wait_send()
 
-    for step in range(R):
-        w_right(step).wait_send()
-        gw_right(step).wait_send()
-    for step in range(L):
-        w_left(step).wait_send()
-        gw_left(step).wait_send()
+    for direction in range(2):
+        for half in range(2):
+            for step in range(long_way(direction, half)):
+                w_copy(direction, half, step).wait_send()
+                gw_copy(direction, half, step).wait_send()
     for pair in pairs:
         unless_self(pair, lambda: cot_copy(pair).wait_send())
-        unless_self(pair, lambda: out_copy(pair).wait_send())
+    if NK == 2:
+        pair_copy().wait_send()
+    for d in range(1, NX):
+        outx_copy(d).wait_send()
+    for d in range(1, NY):
+        outy_copy(d).wait_send()
     for d in range(1, NY):
         g_copy(d).wait_send()
         up_copy(d).wait_send()
@@ -698,7 +745,6 @@
     OT = out_cotangent.shape[1]
     OY = NZ * ROWS
     R = NZ // 2
-    L = max(NZ - 1 - R, 1)
     vmem = pltpu.VMEM
     dma = pltpu.SemaphoreType.DMA
     whole = pl.BlockSpec(memory_space=pltpu.VMEM)
@@ -732,10 +778,13 @@
         vmem((NY * ROWS, C), BF16),
         vmem((NY, ROWS, C), BF16),
         vmem((NY * ROWS, OY), BF16),
-        vmem((NX * NK, ROWS, OT), BF16),
+        vmem((NY * ROWS, OT), BF16),
+        vmem((NY * ROWS, OT), BF16),
+        vmem((NY, ROWS, OT), BF16),
+        vmem((NX, ROWS, OT), BF16),
         vmem((NZ, ROWS, C), BF16),
-        vmem((R, ROWS, C), BF16),
-        vmem((L, ROWS, C), BF16),
+        vmem((2, R, HALF, C), BF16),
+        vmem((2, R, HALF, C), BF16),
         vmem((3, ROWS + 8, C), F32),
         vmem((24, C), F32),
         vmem((32, LANES), F32),
@@ -744,17 +793,18 @@
         dma((2,)),
         dma((NX, NK)),
         dma((NY, NK)),
-        dma((2, R)),
-        dma((2, L)),
+        dma((2, 2, R)),
+        dma((2, 2, R)),
         dma((2, 2, NZ)),
         dma((2, 2, NY)),
         dma((2, 2, NZ)),
         dma((2, NY)),
         dma((2, NY)),
-        dma((NY, NK)),
-        dma((NX, NK)),
-        dma((2, R)),
-        dma((2, L)),
+        dma((2,)),
+        dma((2, NY)),
+        dma((2, NX)),
+        dma((2, 2, R)),
+        dma((2, 2, R)),
         dma((2,)),
         dma((2, NZ)),
         dma((2, NY)),

time: 136 us -> 104 us (0.76)
  Pallas kernels: 130 us -> 97.8 us
    pallas_call x1, Pallas kernels: 130 us -> 97.8 us  [shards(): pl.pallas_call(functools.partial(kernel, dims), out_shape=(jax.ShapeDtype...]
where the time goes in v2:
time: 104 us
  Pallas kernels  97.8 us (94%)
  local copies, waits for them, and re-layouts  5.76 us (6%)
    pallas_call x1, Pallas kernels, shards(): pl.pallas_call(functools.partial(kernel, dims), out_shape=(jax.ShapeDtype...  97.8 us
    unnamed x11, local copies, waits for them, and re-layouts  5.76 us

profile of v2, /device:TPU:4, one launch (start us, length us, event | category | flops | bytes accessed | tf_op | source)
XLA Modules:
  0.0 104.2 jit_solution(15709565969898088106)
XLA Ops:
  0.6 97.8 %mixer.1 = (bf16[128,512]{1,0:T(8,128)(2,1)}, bf16[3,128,1024]{2,1,0:T(8,128)(2,1)}, f32[3,7,64]{2,1,0:T(8,128)}, f32[1,1024]{1,0:T(1,128)}, f32[128,1024]{1,0:T(8,128)}) custom-call(bf16[3,128,1024]{2,1,0:T(8,128)(2,1)} %s_ref.1, f32[3,7,64]{2,1,0:T(8,128)} %sf_ref.1, f32[16,64]{1,0:T(8,128)} %res_ref.1, f32[16,64]{1,0:T(8,128)} %rate_ref.1, ...), custom_call_target="tpu_custom_call" | custom-call | tf_op jit(solution)/shard_map/mixer/pallas_call | solution.py:812
  98.4 1.6 %copy.17 = bf16[128,512]{1,0:T(8,128)(2,1)} copy(bf16[128,512]{1,0:T(8,128)(2,1)} %get-tuple-element.20) | data formatting | bytes 262144
  100.0 0.0 copy-start.1
  100.0 0.0 copy-start
  100.0 2.1 %copy.18 = bf16[3,128,1024]{2,1,0:T(8,128)(2,1)} copy(bf16[3,128,1024]{2,1,0:T(8,128)(2,1)} %get-tuple-element.21) | data formatting | bytes 1572864
  102.1 0.0 copy-done.1
  102.1 0.0 copy-start.2
  102.1 0.6 copy.19
  102.7 0.1 copy-done.2
  102.8 0.6 copy.20
  103.4 0.0 copy-done
  103.4 0.8 copy.21
Async XLA Ops:
  100.0 2.1 %copy-start.1 = (f32[3,7,64]{2,1,0:T(8,128)S(1)}, f32[3,7,64]{2,1,0:T(8,128)}, u32[]{:S(2)}) copy-start(f32[3,7,64]{2,1,0:T(8,128)} %get-tuple-element.22) | copy-start | bytes 16132
  100.0 3.4 %copy-start = (f32[128,1024]{1,0:T(8,128)S(1)}, f32[128,1024]{1,0:T(8,128)}, u32[]{:S(2)}) copy-start(f32[128,1024]{1,0:T(8,128)} %get-tuple-element.24) | copy-start | bytes 1572868
  102.1 0.7 copy-start.2

commit v3 on v2

--- a/solution.py
+++ b/solution.py
@@ -87,6 +87,7 @@
     rim_sem,
     cot_s,
     cot_r,
+    cotp_sem,
     wr_sem,
     wl_sem,
     stz_sem,
@@ -109,6 +110,7 @@
     OT = cot_ref.shape[1]
     OY = NZ * ROWS
     R = NZ // 2
+    HC = C // 2
     c = lax.axis_index("ctx")
     p = lax.axis_index("tp")
     y, z = lax.div(c, NZ), lax.rem(c, NZ)
@@ -132,13 +134,11 @@
     def lanes_of(tile, width=LANES):
         return pl.ds(pl.multiple_of(tile * width, width), width)
 
-    def unless_self(pair, body):
-        if pair == (0, 0):
+    def unless_self(distance, body):
+        if distance == 0:
             pl.when(x != y)(body)
         else:
             body()
-
-    pairs = [(a, b) for a in range(NX) for b in range(NK)]
 
     barrier = pltpu.get_barrier_semaphore()
 
@@ -153,9 +153,9 @@
         greet(dev(y, z, plus(x, d, NX)))
     for d in range(1, NK):
         greet(dev(y, z, x, plus(k, d, NK)))
-    for pair in pairs:
-        unless_self(pair, lambda: greet(dev(x, z, plus(x, pair[0], NX), plus(k, pair[1], NK))))
-        unless_self(pair, lambda: greet(dev(plus(y, pair[0], NY), z, y, plus(k, pair[1], NK))))
+    for d in range(NX):
+        unless_self(d, lambda: greet(dev(x, z, plus(x, d, NX))))
+        unless_self(d, lambda: greet(dev(plus(y, d, NY), z, y)))
 
     @pl.when(c > 0)
     def _():
@@ -225,12 +225,7 @@
             tf[j, :, pl.ds(g * LANES, LANES)] = jnp.where(lane_id <= row_id, skew, 0.0).astype(BF16)
         return carry
 
-    lax.fori_loop(0, NZ, tables, 0)
-
-    for i in range(3):
-        xpad[i, pl.ds(8, ROWS), :] = s_ref[i].astype(F32)
-
-    peers = NZ - 1 + NY - 1 + NX - 1 + NK - 1 + 2 * (NX * NK - 1)
+    peers = NZ - 1 + NY - 1 + NX - 1 + NK - 1 + 2 * (NX - 1)
     peers = peers + jnp.where(x != y, 2, 0) + jnp.where(c > 0, 1, 0) + jnp.where(c < last, 1, 0)
     pl.semaphore_wait(barrier, peers)
 
@@ -273,23 +268,26 @@
             if long_way(direction, half) > 0:
                 w_copy(direction, half, 0).start()
 
-    def cot_copy(pair):
+    def cot_copy(d):
         return remote(
-            cot_ref,
-            cotg.at[rows_of(y), lanes_of(k, OT)],
-            cot_s.at[pair[0], pair[1]],
-            cot_r.at[y, k],
-            dev(x, z, plus(x, pair[0], NX), plus(k, pair[1], NK)),
+            cot_ref, cotg.at[rows_of(y), lanes_of(k, OT)], cot_s.at[d], cot_r.at[y], dev(x, z, plus(x, d, NX))
         )
 
-    for pair in pairs:
-        unless_self(pair, lambda: cot_copy(pair).start())
+    def cot_pair():
+        block = cotg.at[:, lanes_of(k, OT)]
+        return remote(block, block, cotp_sem.at[0], cotp_sem.at[1], dev(y, z, x, 1 - k))
+
+    for d in range(NX):
+        unless_self(d, lambda: cot_copy(d).start())
 
     @pl.when(x == y)
     def _():
         cotg[rows_of(y), lanes_of(k, OT)] = cot_ref[...]
 
-    lax.fori_loop(0, NZ, toeplitz, 0)
+    lax.fori_loop(0, NZ, tables, 0)
+
+    for i in range(3):
+        xpad[i, pl.ds(8, ROWS), :] = s_ref[i].astype(F32)
 
     @pl.when(c == 0)
     def _():
@@ -397,6 +395,8 @@
     lax.fori_loop(0, NZ, smooth, 0)
     states_out(0)
     w_arrived(1, 0)
+    lax.fori_loop(0, NZ, toeplitz, 0)
+    w_arrived(1, 1)
 
     def local_field(j, carry):
         ls = lanes_of(j)
@@ -407,17 +407,22 @@
         return carry
 
     lax.fori_loop(0, R, local_field, 0)
-    w_arrived(1, 1)
+    w_arrived(2, 0)
+    states_row(0)
     lax.fori_loop(R, NZ, local_field, 0)
-    for step, lap in [(2, 0)]:
-        w_arrived(step, lap)
-    states_row(0)
-    for step, lap in [(2, 1), (3, 0)]:
-        w_arrived(step, lap)
+    w_arrived(2, 1)
     states_back(0)
-    for step, lap in [(3, 1)] + [(n, lap) for n in range(4, R + 1) for lap in range(2)]:
-        w_arrived(step, lap)
-    states_in(0)
+    w_arrived(3, 0)
+    for a in range(NY):
+
+        def cot_wait():
+            block = cotg.at[pl.ds(a * ROWS, ROWS), lanes_of(k, OT)]
+            remote(block, block, cot_s.at[0], cot_r.at[a], right).wait_recv()
+
+        pl.when(jnp.logical_not((x == y) & (y == a)))(cot_wait)
+    if NK == 2:
+        cot_pair().start()
+    w_arrived(3, 1)
 
     def gate(j, carry):
         ls = lanes_of(j)
@@ -426,24 +431,28 @@
         gg[rows_of(y), ls] = (sm[0, :, ls] * value).astype(BF16)
         return carry
 
-    lax.fori_loop(0, NZ, gate, 0)
-
-    def g_copy(d):
-        return remote(
-            gg.at[rows_of(y), :], gg.at[rows_of(y), :], g_sem.at[0, d], g_sem.at[1, d], dev(plus(y, d, NY), z)
-        )
-
-    for d in range(1, NY):
-        g_copy(d).start()
-
-    for a in range(NY):
-        for b in range(NK):
-
-            def cot_wait():
-                block = cotg.at[pl.ds(a * ROWS, ROWS), pl.ds(b * OT, OT)]
-                remote(block, block, cot_s.at[0, 0], cot_r.at[a, b], dev(y, z)).wait_recv()
-
-            pl.when(jnp.logical_not((x == y) & (y == a) & (k == b)))(cot_wait)
+    def g_copy(d, half):
+        block = gg.at[rows_of(y), pl.ds(half * HC, HC)]
+        return remote(block, block, g_sem.at[0, half, d], g_sem.at[1, half, d], dev(plus(y, d, NY), z))
+
+    def gate_half(half):
+        lax.fori_loop(half * (NZ // 2), (half + 1) * (NZ // 2), gate, 0)
+        for d in range(1, NY):
+            g_copy(d, half).start()
+
+    def g_arrived(half):
+        for d in range(1, NY):
+            block = gg.at[rows_of(plus(y, -d, NY)), pl.ds(half * HC, HC)]
+            remote(block, block, g_sem.at[0, half, d], g_sem.at[1, half, d], right).wait_recv()
+
+    states_in(0)
+    gate_half(0)
+    for n in range(4, R + 1):
+        for lap in range(2):
+            w_arrived(n, lap)
+    if NK == 2:
+        other = cotg.at[:, lanes_of(1 - k, OT)]
+        remote(other, other, cotp_sem.at[0], cotp_sem.at[1], right).wait_recv()
 
     WIDE = 256
 
@@ -461,19 +470,19 @@
     for d in range(1, NY):
         up_copy(d).start()
 
-    for d in range(1, NY):
-        src = plus(y, -d, NY)
-        block = gg.at[rows_of(src), :]
-        remote(block, block, g_sem.at[0, d], g_sem.at[1, d], dev(src, z)).wait_recv()
+    gate_half(1)
 
     over_rows = (((0,), (0,)), ((), ()))
 
-    def gw_part(i, carry):
-        block = lax.rem(z + R + NZ - i, NZ)
-        gwp[block] = lax.dot_general(
-            cotg[:, lanes_of(block)], gg[...], over_rows, preferred_element_type=F32
-        ).astype(BF16)
-        return carry
+    def gw_part(half):
+        def body(i, carry):
+            block = lax.rem(z + R + NZ - i, NZ)
+            gwp[block, :, pl.ds(half * HC, HC)] = lax.dot_general(
+                cotg[:, lanes_of(block)], gg[:, pl.ds(half * HC, HC)], over_rows, preferred_element_type=F32
+            ).astype(BF16)
+            return carry
+
+        lax.fori_loop(0, NZ, body, 0)
 
     def gw_block(direction, half, step):
         far = long_way(direction, half) - step
@@ -482,30 +491,29 @@
     def gw_copy(direction, half, step):
         sem, into = (gwr_sem, gw_r) if direction == 0 else (gwl_sem, gw_l)
         return remote(
-            gwp.at[gw_block(direction, half, step), pl.ds(half * HALF, HALF), :],
+            gwp.at[gw_block(direction, half, step), :, pl.ds(half * HC, HC)],
             into.at[half, step],
             sem.at[0, half, step],
             sem.at[1, half, step],
             right if direction == 0 else left,
         )
 
-    def gw_arrived(step, lap):
+    def gw_arrived(step, half):
+        cols = pl.ds(half * HC, HC)
         for direction in range(2):
-            half = direction if lap == 0 else 1 - direction
             steps = long_way(direction, half)
             if step <= steps:
                 gw_copy(direction, half, step - 1).wait_recv()
             if step < steps:
                 at = gw_block(direction, half, step)
                 came = gw_r if direction == 0 else gw_l
-                rows = pl.ds(half * HALF, HALF)
-                gwp[at, rows, :] = (gwp[at, rows, :].astype(F32) + came[half, step - 1].astype(F32)).astype(BF16)
+                gwp[at, :, cols] = (gwp[at, :, cols].astype(F32) + came[half, step - 1].astype(F32)).astype(BF16)
                 gw_copy(direction, half, step).start()
 
-    lax.fori_loop(0, NZ, gw_part, 0)
-    for lap in range(2):
+    def gw_start(half):
+        g_arrived(half)
+        gw_part(half)
         for direction in range(2):
-            half = direction if lap == 0 else 1 - direction
             if long_way(direction, half) > 0:
                 gw_copy(direction, half, 0).start()
 
@@ -514,7 +522,6 @@
         outp[:, ls] = lax.dot_general(gg[...], wg[ls, :], turned, preferred_element_type=F32).astype(BF16)
         return carry
 
-    lax.fori_loop(0, OY // WIDE, out_part, 0)
 
     def pair_copy():
         return remote(
@@ -528,9 +535,6 @@
     def outx_copy(d):
         to = plus(x, d, NX)
         return remote(out_y.at[to], out_x.at[x], outx_sem.at[0, d], outx_sem.at[1, d], dev(y, z, to))
-
-    if NK == 2:
-        pair_copy().start()
 
     def out_over_y():
         if NK == 2:
@@ -559,9 +563,8 @@
             value = value + out_x[n].astype(F32)
         out_ref[...] = value.astype(BF16)
 
+    gw_start(0)
     gw_arrived(1, 0)
-    out_over_y()
-    gw_arrived(1, 1)
 
     for d in range(1, NY):
         up_copy(d).wait_recv()
@@ -600,29 +603,23 @@
 
     gw_arrived(2, 0)
     lax.fori_loop(0, NZ, local_grad, 0)
-    gw_arrived(2, 1)
-    out_over_x()
+    gw_start(1)
     states_row(1)
+    lax.fori_loop(0, OY // WIDE, out_part, 0)
+    if NK == 2:
+        pair_copy().start()
     gw_arrived(3, 0)
+    states_back(1)
+    gw_arrived(1, 1)
+    for n in range(4, R + 1):
+        gw_arrived(n, 0)
 
     def first_taps(j, carry):
         tap_grad(0, j)
         return carry
 
     lax.fori_loop(0, NZ, first_taps, 0)
-    states_back(1)
-    gw_arrived(3, 1)
-    out_done()
-    for n in range(4, R + 1):
-        for lap in range(2):
-            gw_arrived(n, lap)
-    for half in range(2):
-        rows = pl.ds(half * HALF, HALF)
-        mine = gwp[z, rows, :].astype(F32)
-        for direction, came in ((0, gw_r), (1, gw_l)):
-            if long_way(direction, half) > 0:
-                mine = mine + came[half, long_way(direction, half) - 1].astype(F32)
-        gw_ref[rows, :] = mine
+    out_over_y()
     states_in(1)
 
     def grad_mixed(j, carry):
@@ -651,6 +648,7 @@
         tap_grad(2, j)
         return carry
 
+    gw_arrived(2, 1)
     lax.fori_loop(0, NZ, other_taps, 0)
     tapsum[pl.ds(3 * TAPS, 3), :] = jnp.zeros((3, C), F32)
     gather_groups = (lax.div(iota((C, LANES), 0), MEMBERS) == iota((C, LANES), 1)).astype(F32)
@@ -684,6 +682,8 @@
             gs_ref[i, :, ls] = total.astype(BF16)
         return carry
 
+    out_over_x()
+    gw_arrived(3, 1)
     lax.fori_loop(0, NZ, streams_grad, 0)
 
     total = sml[...]
@@ -693,6 +693,17 @@
     smy[0] = total
     for d in range(1, NY):
         small_y(d).start()
+
+    out_done()
+    for n in range(4, R + 1):
+        gw_arrived(n, 1)
+    for half in range(2):
+        cols = pl.ds(half * HC, HC)
+        mine = gwp[z, :, cols].astype(F32)
+        for direction, came in ((0, gw_r), (1, gw_l)):
+            if long_way(direction, half) > 0:
+                mine = mine + came[half, long_way(direction, half) - 1].astype(F32)
+        gw_ref[:, cols] = mine
 
     total = smy[0]
     for d in range(1, NY):
@@ -716,16 +727,18 @@
             for step in range(long_way(direction, half)):
                 w_copy(direction, half, step).wait_send()
                 gw_copy(direction, half, step).wait_send()
-    for pair in pairs:
-        unless_self(pair, lambda: cot_copy(pair).wait_send())
+    for d in range(NX):
+        unless_self(d, lambda: cot_copy(d).wait_send())
     if NK == 2:
+        cot_pair().wait_send()
         pair_copy().wait_send()
     for d in range(1, NX):
         outx_copy(d).wait_send()
     for d in range(1, NY):
         outy_copy(d).wait_send()
     for d in range(1, NY):
-        g_copy(d).wait_send()
+        g_copy(d, 0).wait_send()
+        g_copy(d, 1).wait_send()
         up_copy(d).wait_send()
         small_y(d).wait_send()
         for way in range(2):
@@ -736,6 +749,14 @@
             for buf, sem in ((st_out, stz_sem), (ret_out, bef_sem)):
                 block = buf.at[way, plus(z, d, NZ)]
                 remote(block, block, sem.at[way, 0, d], sem.at[way, 1, d], right).wait_send()
+
+
+def hand_over(*refs):
+    copies = [pltpu.make_async_copy(refs[i], refs[5 + i], refs[10].at[i]) for i in range(5)]
+    for one in copies:
+        one.start()
+    for one in copies:
+        one.wait()
 
 
 def shards(dims, streams, short_filter, residues, rates, skip, out_weight, out_cotangent):
@@ -783,22 +804,23 @@
         vmem((NY, ROWS, OT), BF16),
         vmem((NX, ROWS, OT), BF16),
         vmem((NZ, ROWS, C), BF16),
-        vmem((2, R, HALF, C), BF16),
-        vmem((2, R, HALF, C), BF16),
+        vmem((2, R, ROWS, C // 2), BF16),
+        vmem((2, R, ROWS, C // 2), BF16),
         vmem((3, ROWS + 8, C), F32),
         vmem((24, C), F32),
         vmem((32, LANES), F32),
         vmem((NZ, 32, LANES), F32),
         vmem((NY, 32, LANES), F32),
         dma((2,)),
-        dma((NX, NK)),
-        dma((NY, NK)),
+        dma((NX,)),
+        dma((NY,)),
+        dma((2,)),
         dma((2, 2, R)),
         dma((2, 2, R)),
         dma((2, 2, NZ)),
         dma((2, 2, NY)),
         dma((2, 2, NZ)),
-        dma((2, NY)),
+        dma((2, 2, NY)),
         dma((2, NY)),
         dma((2,)),
         dma((2, NY)),
@@ -826,6 +848,15 @@
         ),
         name="mixer",
     )(streams, short_filter, residues, rates, skip.reshape(1, C), out_weight, out_cotangent)
+    results = (output, grad_streams, grad_short, grad_skip, grad_weight)
+    output, grad_streams, grad_short, grad_skip, grad_weight = pl.pallas_call(
+        hand_over,
+        out_shape=tuple(jax.ShapeDtypeStruct(a.shape, a.dtype) for a in results),
+        in_specs=[whole] * 5,
+        out_specs=(pl.BlockSpec(memory_space=pl.ANY),) * 5,
+        scratch_shapes=[dma((5,))],
+        name="hand_over",
+    )(*results)
     return output, grad_streams, grad_short, grad_skip.reshape(C), grad_weight
 
 

time: 104 us -> 91.8 us (0.88)
  Pallas kernels: 97.8 us -> 90.8 us
  local copies, waits for them, and re-layouts: 5.76 us -> 0 us
    pallas_call x1, Pallas kernels: 97.8 us -> 88.3 us  [shards(): pl.pallas_call(functools.partial(kernel, dims), out_shape=(jax.ShapeDtype...]
    unnamed x11 -> x0, local copies, waits for them, and re-layouts: 5.76 us -> none
    pallas_call x0 -> x1, Pallas kernels: none -> 2.49 us  [shards(): pl.pallas_call(hand_over, out_shape=tuple((jax.ShapeDtypeStruct(a.shape,...]
where the time goes in v3:
time: 91.8 us; the launch traced here: 91.5 us
  Pallas kernels  90.8 us (99%)
    pallas_call x1, Pallas kernels, shards(): pl.pallas_call(functools.partial(kernel, dims), out_shape=(jax.ShapeDtype...  88.3 us
    pallas_call x1, Pallas kernels, shards(): pl.pallas_call(hand_over, out_shape=tuple((jax.ShapeDtypeStruct(a.shape,...  2.49 us

profile of v3, /device:TPU:4, one launch (start us, length us, event | category | flops | bytes accessed | tf_op | source)
XLA Modules:
  0.0 91.5 jit_solution(3833619349708424341)
XLA Ops:
  0.6 88.3 %mixer.1 = (bf16[128,512]{1,0:T(8,128)(2,1)}, bf16[3,128,1024]{2,1,0:T(8,128)(2,1)}, f32[3,7,64]{2,1,0:T(8,128)}, f32[1,1024]{1,0:T(1,128)}, f32[128,1024]{1,0:T(8,128)}) custom-call(bf16[3,128,1024]{2,1,0:T(8,128)(2,1)} %s_ref.1, f32[3,7,64]{2,1,0:T(8,128)} %sf_ref.1, f32[16,64]{1,0:T(8,128)} %res_ref.1, f32[16,64]{1,0:T(8,128)} %rate_ref.1, ...), custom_call_target="tpu_custom_call" | custom-call | tf_op jit(solution)/shard_map/mixer/pallas_call | solution.py:834
  89.0 2.5 %hand_over.1 = (bf16[128,512]{1,0:T(8,128)(2,1)}, bf16[3,128,1024]{2,1,0:T(8,128)(2,1)}, f32[3,7,64]{2,1,0:T(8,128)}, f32[1,1024]{1,0:T(1,128)}, f32[128,1024]{1,0:T(8,128)}) custom-call(bf16[128,512]{1,0:T(8,128)(2,1)} %get-tuple-element.15.refs_0_, bf16[3,128,1024]{2,1,0:T(8,128)(2,1)} %get-tuple-element.16.refs_1_, ...), custom_call_target="tpu_custom_call" | custom-call | tf_op jit(solution)/shard_map/hand_over/pallas_call | solution.py:852

commit v4 on v3

--- a/solution.py
+++ b/solution.py
@@ -407,11 +407,11 @@
         return carry
 
     lax.fori_loop(0, R, local_field, 0)
+    states_row(0)
     w_arrived(2, 0)
-    states_row(0)
     lax.fori_loop(R, NZ, local_field, 0)
+    states_back(0)
     w_arrived(2, 1)
-    states_back(0)
     w_arrived(3, 0)
     for a in range(NY):
 
@@ -488,34 +488,39 @@
         far = long_way(direction, half) - step
         return plus(z, far if direction == 0 else -far, NZ)
 
-    def gw_copy(direction, half, step):
+    def gw_copy(direction, half, step, part):
         sem, into = (gwr_sem, gw_r) if direction == 0 else (gwl_sem, gw_l)
+        rows = pl.ds(part * HALF, HALF)
         return remote(
-            gwp.at[gw_block(direction, half, step), :, pl.ds(half * HC, HC)],
-            into.at[half, step],
-            sem.at[0, half, step],
-            sem.at[1, half, step],
+            gwp.at[gw_block(direction, half, step), rows, pl.ds(half * HC, HC)],
+            into.at[half, step, rows, :],
+            sem.at[0, half, step, part],
+            sem.at[1, half, step, part],
             right if direction == 0 else left,
         )
 
     def gw_arrived(step, half):
         cols = pl.ds(half * HC, HC)
-        for direction in range(2):
-            steps = long_way(direction, half)
-            if step <= steps:
-                gw_copy(direction, half, step - 1).wait_recv()
-            if step < steps:
-                at = gw_block(direction, half, step)
-                came = gw_r if direction == 0 else gw_l
-                gwp[at, :, cols] = (gwp[at, :, cols].astype(F32) + came[half, step - 1].astype(F32)).astype(BF16)
-                gw_copy(direction, half, step).start()
+        for part in range(2):
+            rows = pl.ds(part * HALF, HALF)
+            for direction in range(2):
+                steps = long_way(direction, half)
+                if step <= steps:
+                    gw_copy(direction, half, step - 1, part).wait_recv()
+                if step < steps:
+                    at = gw_block(direction, half, step)
+                    came = gw_r if direction == 0 else gw_l
+                    mine = gwp[at, rows, cols].astype(F32)
+                    gwp[at, rows, cols] = (mine + came[half, step - 1, rows, :].astype(F32)).astype(BF16)
+                    gw_copy(direction, half, step, part).start()
 
     def gw_start(half):
         g_arrived(half)
         gw_part(half)
         for direction in range(2):
             if long_way(direction, half) > 0:
-                gw_copy(direction, half, 0).start()
+                for part in range(2):
+                    gw_copy(direction, half, 0, part).start()
 
     def out_part(j, carry):
         ls = lanes_of(j, WIDE)
@@ -726,7 +731,8 @@
         for half in range(2):
             for step in range(long_way(direction, half)):
                 w_copy(direction, half, step).wait_send()
-                gw_copy(direction, half, step).wait_send()
+                gw_copy(direction, half, step, 0).wait_send()
+                gw_copy(direction, half, step, 1).wait_send()
     for d in range(NX):
         unless_self(d, lambda: cot_copy(d).wait_send())
     if NK == 2:
@@ -825,8 +831,8 @@
         dma((2,)),
         dma((2, NY)),
         dma((2, NX)),
-        dma((2, 2, R)),
-        dma((2, 2, R)),
+        dma((2, 2, R, 2)),
+        dma((2, 2, R, 2)),
         dma((2,)),
         dma((2, NZ)),
         dma((2, NY)),

time: 91.8 us -> 91.1 us (level)
  no operation moved by 1% of the time
where the time goes in v4:
time: 91.1 us; the launch traced here: 90.7 us
  Pallas kernels  90.1 us (99%)
    pallas_call x1, Pallas kernels, shards(): pl.pallas_call(functools.partial(kernel, dims), out_shape=(jax.ShapeDtype...  87.6 us
    pallas_call x1, Pallas kernels, shards(): pl.pallas_call(hand_over, out_shape=tuple((jax.ShapeDtypeStruct(a.shape,...  2.49 us

profile of v4, /device:TPU:4, one launch (start us, length us, event | category | flops | bytes accessed | tf_op | source)
XLA Modules:
  0.0 90.7 jit_solution(4639037564349341323)
XLA Ops:
  0.6 87.6 %mixer.1 = (bf16[128,512]{1,0:T(8,128)(2,1)}, bf16[3,128,1024]{2,1,0:T(8,128)(2,1)}, f32[3,7,64]{2,1,0:T(8,128)}, f32[1,1024]{1,0:T(1,128)}, f32[128,1024]{1,0:T(8,128)}) custom-call(bf16[3,128,1024]{2,1,0:T(8,128)(2,1)} %s_ref.1, f32[3,7,64]{2,1,0:T(8,128)} %sf_ref.1, f32[16,64]{1,0:T(8,128)} %res_ref.1, f32[16,64]{1,0:T(8,128)} %rate_ref.1, ...), custom_call_target="tpu_custom_call" | custom-call | tf_op jit(solution)/shard_map/mixer/pallas_call | solution.py:840
  88.2 2.5 %hand_over.1 = (bf16[128,512]{1,0:T(8,128)(2,1)}, bf16[3,128,1024]{2,1,0:T(8,128)(2,1)}, f32[3,7,64]{2,1,0:T(8,128)}, f32[1,1024]{1,0:T(1,128)}, f32[128,1024]{1,0:T(8,128)}) custom-call(bf16[128,512]{1,0:T(8,128)(2,1)} %get-tuple-element.15.refs_0_, bf16[3,128,1024]{2,1,0:T(8,128)(2,1)} %get-tuple-element.16.refs_1_, ...), custom_call_target="tpu_custom_call" | custom-call | tf_op jit(solution)/shard_map/hand_over/pallas_call | solution.py:858

commit v5 on v4

--- a/solution.py
+++ b/solution.py
@@ -758,11 +758,17 @@
 
 
 def hand_over(*refs):
-    copies = [pltpu.make_async_copy(refs[i], refs[5 + i], refs[10].at[i]) for i in range(5)]
-    for one in copies:
-        one.start()
-    for one in copies:
-        one.wait()
+    ins, outs, held, sem = refs[:5], refs[5:10], refs[10:15], refs[15]
+    loads = [pltpu.make_async_copy(ins[i], held[i], sem.at[0, i]) for i in range(5)]
+    stores = [pltpu.make_async_copy(held[i], outs[i], sem.at[1, i]) for i in range(5)]
+    order = (4, 1, 0, 2, 3)
+    for i in order:
+        loads[i].start()
+    for i in order:
+        loads[i].wait()
+        stores[i].start()
+    for i in order:
+        stores[i].wait()
 
 
 def shards(dims, streams, short_filter, residues, rates, skip, out_weight, out_cotangent):
@@ -858,9 +864,9 @@
     output, grad_streams, grad_short, grad_skip, grad_weight = pl.pallas_call(
         hand_over,
         out_shape=tuple(jax.ShapeDtypeStruct(a.shape, a.dtype) for a in results),
-        in_specs=[whole] * 5,
+        in_specs=[pl.BlockSpec(memory_space=pl.ANY)] * 5,
         out_specs=(pl.BlockSpec(memory_space=pl.ANY),) * 5,
-        scratch_shapes=[dma((5,))],
+        scratch_shapes=[vmem(a.shape, a.dtype) for a in results] + [dma((2, 5))],
         name="hand_over",
     )(*results)
     return output, grad_streams, grad_short, grad_skip.reshape(C), grad_weight

time: 91.1 us -> 90.9 us (level)
  no operation moved by 1% of the time
where the time goes in v5:
time: 90.9 us; the launch traced here: 90.5 us
  Pallas kernels  89.9 us (99%)
    pallas_call x1, Pallas kernels, shards(): pl.pallas_call(functools.partial(kernel, dims), out_shape=(jax.ShapeDtype...  87.6 us
    pallas_call x1, Pallas kernels, shards(): pl.pallas_call(hand_over, out_shape=tuple((jax.ShapeDtypeStruct(a.shape,...  2.3 us

profile of v5, /device:TPU:4, one launch (start us, length us, event | category | flops | bytes accessed | tf_op | source)
XLA Modules:
  0.0 90.5 jit_solution(7127839572885968218)
XLA Ops:
  0.6 87.6 %mixer.1 = (bf16[128,512]{1,0:T(8,128)(2,1)}, bf16[3,128,1024]{2,1,0:T(8,128)(2,1)}, f32[3,7,64]{2,1,0:T(8,128)}, f32[1,1024]{1,0:T(1,128)}, f32[128,1024]{1,0:T(8,128)}) custom-call(bf16[3,128,1024]{2,1,0:T(8,128)(2,1)} %s_ref.1, f32[3,7,64]{2,1,0:T(8,128)} %sf_ref.1, f32[16,64]{1,0:T(8,128)} %res_ref.1, f32[16,64]{1,0:T(8,128)} %rate_ref.1, ...), custom_call_target="tpu_custom_call" | custom-call | tf_op jit(solution)/shard_map/mixer/pallas_call | solution.py:846
  88.2 2.3 %hand_over.1 = (bf16[128,512]{1,0:T(8,128)(2,1)}, bf16[3,128,1024]{2,1,0:T(8,128)(2,1)}, f32[3,7,64]{2,1,0:T(8,128)}, f32[1,1024]{1,0:T(1,128)}, f32[128,1024]{1,0:T(8,128)}) custom-call(bf16[128,512]{1,0:T(8,128)(2,1)} %get-tuple-element.15.refs_0_, bf16[3,128,1024]{2,1,0:T(8,128)(2,1)} %get-tuple-element.16.refs_1_, ...), custom_call_target="tpu_custom_call" | custom-call | tf_op jit(solution)/shard_map/hand_over/pallas_call | solution.py:864
